TPU v7x, 256 devices: a whole 4x4x8 slice. The times are simulated.
256 devices in a mesh: grp: 16 (over z, core), ing: 16 (over y, x).
Axes of the slice: x: 4, y: 4, z: 8, core: 2. Of those that a mesh axis runs over, the one named last changes fastest.
Arguments:
- amplitudes: bfloat16 [512, 800, 800], P('grp', 'ing'), may hold values from -6 to 6
- integrals: bfloat16 [512, 800, 800], P('grp', 'ing'), may hold values from -0.0024414062 to 0.0024414062
- fock_block: bfloat16 [800, 800], P('ing'), may hold values from -0.625 to 0.625
- virtual_irrep: int32 [800], replicated, may hold values from 0 to 7, as said below
- pair_irrep: int32 [512], P(('grp', 'ing')), may hold values from 0 to 7
- pair_energy: float32 [512], P(('grp', 'ing')), may hold values from -4 to -1
- virtual_energy: float32 [800], replicated, may hold values from 0.5 to 4
Outputs:
- update: float32 [512, 800, 800], P('grp', 'ing')
Inputs may be any that keep to these rules, and one draw needn't show every extreme that they name: `virtual_irrep`: the orbitals of one irreducible representation form one contiguous run of 100 plus or minus at most 25 orbitals, and all 8 representations occur.
All inputs are finite; a program needn't handle non-finite values.
Results may differ from a plain program's by a relative error of at most 0.0029.
Values may be sent and summed in bfloat16 or wider, within the bound.
A program may use at most 128 MiB of HBM per device.

v0:
```python
import jax
import jax.numpy as jnp
from jax import lax
from jax.sharding import PartitionSpec as P


def symmetry_mask(values, pair_irrep, virtual_irrep):
    allowed = (
        jnp.bitwise_xor(virtual_irrep[:, None], virtual_irrep[None, :])[None]
        == pair_irrep[:, None, None]
    )
    return jnp.where(allowed, values, jnp.zeros_like(values))


def body(amplitudes, integrals, fock_block, virtual_irrep, pair_irrep, pair_energy, virtual_energy):
    same_irrep = virtual_irrep[:, None] == virtual_irrep[None, :]
    whole_amps, whole_ints = (
        lax.all_to_all(amplitudes, "ing", split_axis=0, concat_axis=1, tiled=True),
        lax.all_to_all(integrals, "ing", split_axis=0, concat_axis=1, tiled=True),
    )
    amp_masked = symmetry_mask(whole_amps, pair_irrep, virtual_irrep)
    int_masked = symmetry_mask(whole_ints, pair_irrep, virtual_irrep)
    partial_value = jnp.einsum(
        "paf,pef->ae", amp_masked, int_masked, preferred_element_type=jnp.float32
    )
    correction = lax.psum(partial_value, ("grp", "ing"))
    fock_full = lax.all_gather(fock_block, "ing", axis=0, tiled=True)
    fock_part = jnp.where(
        same_irrep, fock_full.astype(jnp.float32), jnp.zeros(fock_full.shape, jnp.float32)
    )
    operator_vv = (fock_part + correction).astype(jnp.bfloat16)
    product = jnp.einsum("pae,be->pab", amp_masked, operator_vv, preferred_element_type=jnp.float32)
    denominator = (
        pair_energy[:, None, None] - virtual_energy[None, :, None] - virtual_energy[None, None, :]
    )
    scaled = (product - jnp.swapaxes(product, 1, 2)) / denominator
    return lax.all_to_all(scaled, "ing", split_axis=1, concat_axis=0, tiled=True)


def solution(mesh):
    in_specs = (
        P("grp", "ing", None),
        P("grp", "ing", None),
        P("ing", None),
        P(),
        P(("grp", "ing")),
        P(("grp", "ing")),
        P(),
    )
    out_specs = P("grp", "ing", None)
    return jax.shard_map(body, mesh=mesh, in_specs=in_specs, out_specs=out_specs, check_vma=False)
```

profile of v0, /device:TPU:1, one launch (start us, length us, event | category | flops | bytes accessed | tf_op | source)
XLA Modules:
  0.0 514.9 jit_solution(2653213600742417975)
XLA Ops:
  7.4 4.4 copy.25
  11.8 7.6 %all-to-all-start = ((bf16[32,50,800]{2,1,0:T(8,128)(2,1)}), bf16[32,50,800]{2,1,0:T(8,128)(2,1)S(1)}, u32[]{:S(2)}, u32[]{:S(2)}) async-start(bf16[32,50,800]{2,1,0:T(8,128)(2,1)} %copy.25), calls=%async_computation | async-start | bytes 6422528 | tf_op jit(solution)/shard_map/all_to_all | solution.py:18
  19.4 4.5 copy.27
  23.9 0.0 copy-start.2
  23.9 43.1 %all-to-all-done = bf16[32,50,800]{2,1,0:T(8,128)(2,1)S(1)} async-done(((bf16[32,50,800]{2,1,0:T(8,128)(2,1)}), bf16[32,50,800]{2,1,0:T(8,128)(2,1)S(1)}, u32[]{:S(2)}, u32[]{:S(2)}) %all-to-all-start) | async-done | bytes 2560032 | tf_op jit(solution)/shard_map/all_to_all | solution.py:18
  67.0 4.5 all-to-all-start.1
  71.5 0.0 all-gather.3.cloned.1.call-start
  71.6 0.7 all-gather.3.cloned.1.call-update
  72.2 0.0 all-reduce.2.cloned.1.call-start
  72.3 0.0 copy-done.2
  72.3 1.8 broadcast_xor_fusion
  74.2 3.8 copy.26
  78.0 38.4 %all-to-all-done.1 = bf16[32,50,800]{2,1,0:T(8,128)(2,1)} async-done(((bf16[32,50,800]{2,1,0:T(8,128)(2,1)}), bf16[32,50,800]{2,1,0:T(8,128)(2,1)}, u32[]{:S(2)}, u32[]{:S(2)}) %all-to-all-start.1) | async-done | bytes 2560032 | tf_op jit(solution)/shard_map/all_to_all | solution.py:19
  116.4 0.0 copy-start
  116.4 0.0 copy-start.1
  116.4 0.0 copy-start.4
  116.4 4.3 copy.28
  120.7 0.0 copy-done
  120.7 0.0 copy-done.1
  120.7 0.0 copy-done.4
  120.7 7.2 %compare_select_fusion = (bf16[2,800,800]{2,0,1:T(2,128)(2,1)S(1)}, bf16[2,800,800]{2,0,1:T(2,128)(2,1)S(1)}) fusion(bf16[16,2,50,800]{3,1,2,0:T(2,128)(2,1)S(1)} %copy.28, s32[800,800]{1,0:T(8,128)S(1)} %copy-done, s32[2]{0:T(128)S(1)} %copy-done.4, bf16[16,2,50,800]{3,1,2,0:T(2,128)(2,1)S(1)} %copy-done.1), kind=kLoop, calls=%fused_computation | loop fusion | flops 3840000 | bytes 12800008 | tf_op jit(solution)/shard_map/jit(_where)/select_n | solution.py:12
  127.9 4.8 fusion.6
  132.8 0.0 copy-start.3
  132.8 0.0 copy-start.5
  132.8 0.0 all-reduce.2.cloned.1.call-update
  132.8 0.7 copy-done.3
  133.5 0.0 copy-done.5
  133.5 0.1 broadcast_subtract_fusion
  133.5 8.1 %all-gather.3.cloned.1.call-done = bf16[16,50,800]{2,1,0:T(8,128)(2,1)} async-done(((bf16[1,50,800]{2,1,0:T(8,128)(2,1)}), bf16[16,50,800]{2,1,0:T(8,128)(2,1)}) %all-gather.3.cloned.1.call-update) | async-done | bytes 1280016 | tf_op jit(solution)/shard_map/all_gather | solution.py:27
  141.6 3.0 reshape.63
  144.6 251.9 %all-reduce.2.cloned.1.call-done = f32[800,800]{1,0:T(8,128)} async-done(((f32[800,800]{1,0:T(8,128)}), f32[800,800]{1,0:T(8,128)}) %all-reduce.2.cloned.1.call-update) | async-done | bytes 2560016 | tf_op jit(solution)/shard_map/psum | solution.py:26
  396.5 8.1 %fusion.4 = f32[2,800,800]{2,1,0:T(8,128)} fusion(bf16[2,800,800]{2,0,1:T(2,128)(2,1)S(1)} %get-tuple-element.6, f32[800,800]{1,0:T(8,128)} %all-reduce.2.cloned.1.call-done, f32[800,800]{1,0:T(8,128)} %reshape.63, s32[800]{0:T(1024)S(1)} %copy-done.2), kind=kOutput, calls=%fused_computation.8 | convolution fusion | flops 2050560000 | bytes 12803200 | tf_op jit(solution)/shard_map/pae,be->pab/dot_general | solution.py:32
  404.6 7.1 %copy.32 = f32[2,800,800]{1,2,0:T(8,128)} copy(f32[2,800,800]{2,1,0:T(8,128)} %fusion.4) | data formatting | bytes 10240000 | tf_op jit(solution)/shard_map/pae,be->pab/dot_general | solution.py:32
  411.6 5.1 fusion
  416.8 4.4 copy.33
  421.2 72.8 %all_to_all.54 = f32[2,800,800]{2,0,1:T(2,128)S(1)} all-to-all(f32[2,800,800]{2,0,1:T(2,128)S(1)} %copy.33), channel_id=1, replica_groups=mesh['grp'=16,'ing'=16] {'ing'}, dimensions={1} | all-to-all | bytes 10240000 | tf_op jit(solution)/shard_map/all_to_all | solution.py:37
  494.0 5.7 %copy.34 = f32[16,2,50,800]{3,1,0,2:T(2,128)} copy(f32[16,2,50,800]{3,1,2,0:T(2,128)S(1)} %bitcast.25) | data formatting | bytes 10240000 | tf_op jit(solution)/shard_map/all_to_all | solution.py:37
  499.7 7.8 %all_to_all.50 = f32[32,50,800]{2,0,1:T(8,128)} reshape(f32[16,2,50,800]{3,1,0,2:T(2,128)} %copy.34) | data formatting | bytes 10240000 | tf_op jit(solution)/shard_map/all_to_all | solution.py:37
Async XLA Ops:
  11.8 55.2 %all-to-all-start = ((bf16[32,50,800]{2,1,0:T(8,128)(2,1)}), bf16[32,50,800]{2,1,0:T(8,128)(2,1)S(1)}, u32[]{:S(2)}, u32[]{:S(2)}) async-start(bf16[32,50,800]{2,1,0:T(8,128)(2,1)} %copy.25), calls=%async_computation | async-start | bytes 6422528 | tf_op jit(solution)/shard_map/all_to_all | solution.py:18
  23.9 48.4 %copy-start.2 = (s32[800]{0:T(1024)S(1)}, s32[800]{0:T(1024)}, u32[]{:S(2)}) copy-start(s32[800]{0:T(1024)} %param.10) | copy-start | bytes 9604
  67.0 49.4 %all-to-all-start.1 = ((bf16[32,50,800]{2,1,0:T(8,128)(2,1)}), bf16[32,50,800]{2,1,0:T(8,128)(2,1)}, u32[]{:S(2)}, u32[]{:S(2)}) async-start(bf16[32,50,800]{2,1,0:T(8,128)(2,1)} %copy.27), calls=%async_computation.1 | async-start | bytes 6422528 | tf_op jit(solution)/shard_map/all_to_all | solution.py:19
  71.5 70.1 %all-gather.3.cloned.1.call-start = ((), (), s32[]{:S(2)}) async-start(), calls=%async_computation.4 | async-start | bytes 1705984 | tf_op jit(solution)/shard_map/all_gather | solution.py:27
  72.2 324.3 %all-reduce.2.cloned.1.call-start = ((), (), s32[]{:S(2)}) async-start(), calls=%async_computation.3 | async-start | bytes 5734400 | tf_op jit(solution)/shard_map/psum | solution.py:26
  116.4 4.3 copy-start
  116.4 4.3 copy-start.1
  116.4 4.3 copy-start.4
  132.8 0.7 copy-start.3
  132.8 0.7 copy-start.5
Sparse Core Ops, SparseCore 0:
  75.1 66.4 all-gather.2
Sparse Core Ops, SparseCore 1:
  132.9 263.6 all-reduce.1
where the time goes:
time: 517 us; the launch traced here: 515 us
  waiting for transfers between devices  342 us (66%)
  blocking collectives  72.8 us (14%)
  local copies, waits for them, and re-layouts  45.7 us (9%)
  between operations  14.9 us (3%)
  other arithmetic  14.3 us (3%)
  matrix products  12.9 us (2%)
  starting transfers between devices  12.2 us (2%)
    psum x1, waiting for transfers between devices, body(): correction = lax.psum(partial_value, ('grp', 'ing'))  252 us
    all_to_all x1, blocking collectives, body(): lax.all_to_all(scaled, 'ing', split_axis=1, concat_axis=0, tiled=True)  72.8 us
    all_to_all x1, waiting for transfers between devices, body(): lax.all_to_all(amplitudes, 'ing', split_axis=0, concat_axis=1, tiled=True)  43.1 us
    all_to_all x1, waiting for transfers between devices, body(): lax.all_to_all(integrals, 'ing', split_axis=0, concat_axis=1, tiled=True)  38.4 us
    all_to_all x2, local copies, waits for them, and re-layouts, body(): lax.all_to_all(scaled, 'ing', split_axis=1, concat_axis=0, tiled=True)  13.5 us
  transfers between devices with their start and end apart: 4, of which 4 were waited for; matrix products, arithmetic and copies ran while one was open for 6% of the time, Pallas kernels for 0%

commit v1 on v0

v1 whole, which is shorter than its diff:
```python
import functools

import jax
import jax.numpy as jnp
from jax import lax
from jax.experimental import pallas as pl
from jax.experimental.pallas import tpu as pltpu
from jax.sharding import PartitionSpec as P

NV, LANES, TILES = 800, 128, 7
PADDED = LANES * TILES
ROWS, OWN, GROUP_PAIRS = 50, 2, 32
RING, DEPTH, SIDE = 16, 8, 4
PEERS = 2 * RING
SLICE, SLOT = 25, 32
IN_SLOT, OUT_HALF, OUT_SLOT = 208, 56, 112
MESH = pl.DeviceIdType.MESH
F32, BF16, I32 = jnp.float32, jnp.bfloat16, jnp.int32
NT = (((1,), (1,)), ((), ()))


def tile_of(array, t):
    if t < TILES - 1:
        return array[:, LANES * t : LANES * (t + 1)]
    last = array[:, LANES * t : NV]
    pad = jnp.zeros((array.shape[0], PADDED - NV), array.dtype)
    return jnp.concatenate([last, pad], axis=1)


def main_kernel(
    amps, ints, fock, irrep, energy, pair_irrep, pair_energy,
    result, irreps_out, row_key_out,
    amp_in, int_in, col_key, col_energy, row_key, row_energy, own_key,
    g_send, g_recv, stage, pack_send, pack_recv, nat_a, nat_b, lhs, rhs, int_rhs,
    fock_fold, corr, red_send, red_recv, z_send, z_recv, op_send, op_recv, op_nat,
    inverse, scaled, out_stage, out_send, out_recv,
    amp_sem, int_sem, g_ssem, g_rsem, p_ssem, p_rsem, r_ssem, r_rsem,
    z_ssem, z_rsem, o_ssem, o_rsem, t_ssem, t_rsem,
):
    grp, ing = lax.axis_index("grp"), lax.axis_index("ing")
    z, core = grp // 2, grp % 2
    y, x = ing // SIDE, ing % SIDE
    me = ing * 2 + core

    def plane_peer(k):
        return ((y + k // SIDE) % SIDE) * SIDE + (x + k % SIDE) % SIDE

    def far_peer(k):
        return ((y + 2 + k // SIDE) % SIDE) * SIDE + (x + 2 + k % SIDE) % SIDE

    def on_plane(i, c):
        return (z * 2 + c, i)

    def chunk(j):
        place = pl.ds(OWN * j, OWN)
        return (
            pltpu.make_async_copy(amps.at[place], amp_in.at[place], amp_sem.at[j]),
            pltpu.make_async_copy(ints.at[place], int_in.at[place], int_sem.at[j]),
        )

    def load(k, carry):
        for copy in chunk(plane_peer(k)):
            copy.start()
        return carry

    barrier = pltpu.get_barrier_semaphore()

    def greet(k, carry):
        pl.semaphore_signal(
            barrier, inc=1, device_id=on_plane(plane_peer(k // 2), (core + k) % 2), device_id_type=MESH
        )
        return carry

    def greet_z(k, carry):
        pl.semaphore_signal(
            barrier, inc=1, device_id=(((z + k) % DEPTH) * 2 + core, ing), device_id_type=MESH
        )
        return carry

    lax.fori_loop(1, PEERS, greet, 0)
    lax.fori_loop(1, DEPTH, greet_z, 0)
    lax.fori_loop(0, RING, load, 0)

    for q in range(OWN):
        g_send[q : q + 1, :] = jnp.full((1, LANES), pair_irrep[q], I32)
    g_recv[ing] = g_send[...]

    for t in range(TILES):
        if t < TILES - 1:
            col_key[t : t + 1, :] = irrep[:, LANES * t : LANES * (t + 1)]
        else:
            col_key[t : t + 1, :] = jnp.concatenate(
                [irrep[:, LANES * t : NV], jnp.full((1, PADDED - NV), -1, I32)], axis=1
            )
        col_energy[t : t + 1, :] = tile_of(energy[...], t)
    for t in range(TILES):
        place = slice(LANES * t, LANES * (t + 1))
        keys = jnp.broadcast_to(col_key[t : t + 1, :].astype(F32), (LANES, LANES))
        row_key[place, :] = keys.T.astype(I32)
    own_key[...] = row_key[pl.ds(ROWS * ing, OUT_HALF), :]
    row_key_out[...] = own_key[...]

    pl.semaphore_wait(barrier, PEERS - 1 + DEPTH - 1)

    def g_copy(i, slot, c=None):
        return pltpu.make_async_remote_copy(
            src_ref=g_send, dst_ref=g_recv.at[slot], send_sem=g_ssem.at[i], recv_sem=g_rsem.at[slot],
            device_id=on_plane(i, core), device_id_type=MESH,
        )

    def g_start(k, carry):
        g_copy(plane_peer(k), ing).start()
        return carry

    lax.fori_loop(1, RING, g_start, 0)

    def pack_copy(i, slot):
        return pltpu.make_async_remote_copy(
            src_ref=pack_send.at[i], dst_ref=pack_recv.at[slot], send_sem=p_ssem.at[i],
            recv_sem=p_rsem.at[slot], device_id=on_plane(i, core), device_id_type=MESH,
        )

    def fold_chunk(j):
        keys = own_key[0:ROWS, :]
        for q in range(OWN):
            wanted = keys ^ g_recv[j, q : q + 1, :]
            for which, source in ((0, amp_in), (1, int_in)):
                folded = jnp.zeros((ROWS, LANES), F32)
                for t in range(TILES):
                    if t < TILES - 1:
                        part = source[OWN * j + q, :, LANES * t : LANES * (t + 1)].astype(F32)
                    else:
                        part = source[OWN * j + q, :, LANES * t : NV].astype(F32)
                        part = jnp.concatenate([part, jnp.zeros((ROWS, PADDED - NV), F32)], axis=1)
                    folded = jnp.where(wanted == col_key[t : t + 1, :], part, folded)
                first = ROWS * (which * OWN + q)
                stage[first : first + ROWS, :] = folded
        return stage[...].astype(BF16)

    stage[4 * ROWS : IN_SLOT, :] = jnp.zeros((IN_SLOT - 4 * ROWS, LANES), F32)

    def pack_step(k, carry):
        j = plane_peer(k)
        g_copy(ing, j).wait_recv()
        for copy in chunk(j):
            copy.wait()
        pack_send[j] = fold_chunk(j)
        pack_copy(j, ing).start()
        return carry

    lax.fori_loop(1, RING, pack_step, 0)
    for copy in chunk(ing):
        copy.wait()
    pack_recv[ing] = fold_chunk(ing)

    fock_rows = fock[...].astype(F32)
    fock_keys = own_key[0:ROWS, :]
    folded_fock = jnp.zeros((ROWS, LANES), F32)
    for t in range(TILES):
        folded_fock = jnp.where(fock_keys == col_key[t : t + 1, :], tile_of(fock_rows, t), folded_fock)
    fock_fold[...] = jnp.zeros(fock_fold.shape, F32)
    fock_fold[0:ROWS, :] = folded_fock
    for t in range(TILES):
        place = slice(LANES * t, LANES * (t + 1))
        row_energy[place, :] = jnp.broadcast_to(col_energy[t : t + 1, :], (LANES, LANES)).T
    for q in range(OWN):
        for t in range(TILES):
            place = slice(LANES * t, LANES * (t + 1))
            wanted = row_key[place, :] ^ pair_irrep[q]
            other = jnp.zeros((LANES, LANES), F32)
            for u in range(TILES):
                other = jnp.where(wanted == col_key[u : u + 1, :], col_energy[u : u + 1, :], other)
            inverse[q, place, :] = 1.0 / (pair_energy[q] - row_energy[place, :] - other)
    nat_a[:, NV:PADDED, :] = jnp.zeros((OWN, PADDED - NV, LANES), F32)
    nat_b[:, NV:PADDED, :] = jnp.zeros((OWN, PADDED - NV, LANES), F32)
    op_nat[NV:PADDED, :] = jnp.zeros((PADDED - NV, LANES), F32)
    corr[NV:PADDED, :] = jnp.zeros((PADDED - NV, LANES), F32)

    def unpack(j):
        stage[...] = pack_recv[j].astype(F32)
        place = pl.ds(ROWS * j, ROWS)
        for q in range(OWN):
            nat_a[q, place, :] = stage[ROWS * q : ROWS * (q + 1), :]
            nat_b[q, place, :] = stage[ROWS * (OWN + q) : ROWS * (OWN + q + 1), :]

    unpack(ing)

    def unpack_step(k, carry):
        j = plane_peer(RING - k)
        pack_copy(ing, j).wait_recv()
        unpack(j)
        return carry

    lax.fori_loop(1, RING, unpack_step, 0)

    for q in range(OWN):
        lhs[:, LANES * q : LANES * (q + 1)] = nat_a[q].astype(BF16)
        int_rhs[:, LANES * q : LANES * (q + 1)] = nat_b[q].astype(BF16)
    for r in range(TILES):
        place = slice(LANES * r, LANES * (r + 1))
        low, high = max(r - 1, 0), min(r + 2, TILES)
        block = lax.dot_general(
            lhs[place, :], int_rhs[LANES * low : LANES * high, :], NT, preferred_element_type=F32
        )
        keys = row_key[place, :]
        folded = jnp.zeros((LANES, LANES), F32)
        for t in range(low, high):
            part = block[:, LANES * (t - low) : LANES * (t - low + 1)]
            folded = jnp.where(keys == col_key[t : t + 1, :], part, folded)
        corr[place, :] = folded

    def red_copy(i, c, slot):
        w = i * 2 + c
        return pltpu.make_async_remote_copy(
            src_ref=red_send.at[w], dst_ref=red_recv.at[slot], send_sem=r_ssem.at[w],
            recv_sem=r_rsem.at[slot], device_id=on_plane(i, c), device_id_type=MESH,
        )

    def red_step(k, carry):
        for c in range(2):
            i = far_peer(k)
            w = i * 2 + c
            rows = corr[pl.ds(SLICE * w, SLOT), :]

            @pl.when(w != me)
            def _():
                red_send[w] = rows
                red_copy(i, c, me).start()

            @pl.when(w == me)
            def _():
                red_recv[w] = rows

        return carry

    lax.fori_loop(0, RING, red_step, 0)

    for q in range(OWN):
        rhs[q, :, LANES : 2 * LANES] = (-nat_a[q]).astype(BF16)

    def red_wait(k, carry):
        i, c = plane_peer(k // 2), (core + k) % 2
        red_copy(ing, core, i * 2 + c).wait_recv()
        return carry

    lax.fori_loop(1, PEERS, red_wait, 0)
    total = red_recv[0]
    for w in range(1, PEERS):
        total = total + red_recv[w]
    z_send[...] = total

    def z_copy(dest, slot):
        return pltpu.make_async_remote_copy(
            src_ref=z_send, dst_ref=z_recv.at[slot], send_sem=z_ssem.at[dest],
            recv_sem=z_rsem.at[slot], device_id=(dest * 2 + core, ing), device_id_type=MESH,
        )

    def z_start(k, carry):
        z_copy((z + 3 + k) % DEPTH, z).start()
        return carry

    lax.fori_loop(1, 5, z_start, 0)
    lax.fori_loop(6, 9, z_start, 0)
    z_recv[z] = total

    def z_wait(k, carry):
        z_copy(z, (z + k) % DEPTH).wait_recv()
        return carry

    lax.fori_loop(1, DEPTH, z_wait, 0)
    total = z_recv[0]
    for k in range(1, DEPTH):
        total = total + z_recv[k]
    rows = (fock_fold[pl.ds(SLICE * core, SLOT), :] + total).astype(BF16)
    op_send[...] = rows
    op_recv[me] = rows

    def op_copy(i, c, slot):
        w = i * 2 + c
        return pltpu.make_async_remote_copy(
            src_ref=op_send, dst_ref=op_recv.at[slot], send_sem=o_ssem.at[w],
            recv_sem=o_rsem.at[slot], device_id=on_plane(i, c), device_id_type=MESH,
        )

    def op_start(k, carry):
        for c in range(2):
            i = far_peer(k)

            @pl.when(i * 2 + c != me)
            def _():
                op_copy(i, c, me).start()

        return carry

    lax.fori_loop(0, RING, op_start, 0)

    def op_place(w):
        op_nat[pl.ds(SLICE * w, SLICE), :] = op_recv[w].astype(F32)[0:SLICE, :]

    op_place(me)

    def op_wait(k, carry):
        w = plane_peer(k // 2) * 2 + (core + k) % 2
        op_copy(ing, core, w).wait_recv()
        op_place(w)
        return carry

    lax.fori_loop(1, PEERS, op_wait, 0)

    operator = op_nat[...].astype(BF16)
    for q in range(OWN):
        rhs[q, :, 0:LANES] = operator
        left = jnp.concatenate([lhs[0:NV, LANES * q : LANES * (q + 1)], operator[0:NV, :]], axis=1)
        keys = row_key[0:NV, :] ^ pair_irrep[q]
        folded = jnp.zeros((NV, LANES), F32)
        for t in range(0, TILES, 2):
            width = min(2, TILES - t)
            block = lax.dot_general(
                left, rhs[q, LANES * t : LANES * (t + width), :], NT, preferred_element_type=F32
            )
            for u in range(width):
                part = block[:, LANES * u : LANES * (u + 1)]
                folded = jnp.where(keys == col_key[t + u : t + u + 1, :], part, folded)
        scaled[q, 0:NV, :] = folded * inverse[q, 0:NV, :]

    def out_copy(i, slot):
        return pltpu.make_async_remote_copy(
            src_ref=out_send.at[i], dst_ref=out_recv.at[slot], send_sem=t_ssem.at[i],
            recv_sem=t_rsem.at[slot], device_id=on_plane(i, core), device_id_type=MESH,
        )

    scaled[:, NV:PADDED, :] = jnp.zeros((OWN, PADDED - NV, LANES), F32)

    def out_rows(j):
        for q in range(OWN):
            out_stage[OUT_HALF * q : OUT_HALF * (q + 1), :] = scaled[q, pl.ds(ROWS * j, OUT_HALF), :]
        return out_stage[...].astype(BF16)

    def out_step(k, carry):
        j = far_peer(k)

        @pl.when(j != ing)
        def _():
            out_send[j] = out_rows(j)
            out_copy(j, ing).start()

        return carry

    lax.fori_loop(0, RING, out_step, 0)
    out_recv[ing] = out_rows(ing)
    irreps_out[...] = g_recv[...]

    def sent(k, carry):
        i = plane_peer(k)
        g_copy(i, ing).wait_send()
        pack_copy(i, ing).wait_send()
        return carry

    lax.fori_loop(1, RING, sent, 0)

    def sent_pairs(k, carry):
        i, c = plane_peer(k // 2), (core + k) % 2
        red_copy(i, c, me).wait_send()
        op_copy(i, c, me).wait_send()
        return carry

    lax.fori_loop(1, PEERS, sent_pairs, 0)

    def sent_z(k, carry):
        z_copy((z + k) % DEPTH, z).wait_send()
        return carry

    lax.fori_loop(1, DEPTH, sent_z, 0)

    def out_wait(k, carry):
        j = plane_peer(k)
        out_copy(ing, j).wait_recv()
        out_copy(j, ing).wait_send()
        return carry

    lax.fori_loop(1, RING, out_wait, 0)
    result[...] = out_recv[...]


def expand_kernel(folded, irreps, row_key, irrep, update):
    keys = row_key[0:ROWS, :]
    for b in range(folded.shape[0]):
        values = folded[b].astype(F32)
        for q in range(OWN):
            part = values[OUT_HALF * q : OUT_HALF * q + ROWS, :]
            wanted = keys ^ irreps[b, q : q + 1, :]
            for t in range(TILES):
                width = min(LANES, NV - LANES * t)
                cols = slice(LANES * t, LANES * t + width)
                update[OWN * b + q, :, cols] = jnp.where(
                    wanted[:, 0:width] == irrep[:, cols], part[:, 0:width], 0.0
                )


def body(amplitudes, integrals, fock_block, virtual_irrep, pair_irrep, pair_energy, virtual_energy):
    vmem = pl.BlockSpec(memory_space=pltpu.VMEM)
    smem = pl.BlockSpec(memory_space=pltpu.SMEM)
    hbm = pl.BlockSpec(memory_space=pl.ANY)
    irrep = virtual_irrep.reshape(1, NV)
    dma = pltpu.SemaphoreType.DMA
    result, irreps, row_key = pl.pallas_call(
        main_kernel,
        name="residual",
        out_shape=(
            jax.ShapeDtypeStruct((RING, OUT_SLOT, LANES), BF16),
            jax.ShapeDtypeStruct((RING, OWN, LANES), I32),
            jax.ShapeDtypeStruct((OUT_HALF, LANES), I32),
        ),
        in_specs=[hbm, hbm, vmem, vmem, vmem, smem, smem],
        out_specs=(vmem, vmem, vmem),
        scratch_shapes=[
            pltpu.VMEM((GROUP_PAIRS, ROWS, NV), BF16),
            pltpu.VMEM((GROUP_PAIRS, ROWS, NV), BF16),
            pltpu.VMEM((8, LANES), I32),
            pltpu.VMEM((8, LANES), F32),
            pltpu.VMEM((PADDED, LANES), I32),
            pltpu.VMEM((PADDED, LANES), F32),
            pltpu.VMEM((OUT_HALF, LANES), I32),
            pltpu.VMEM((OWN, LANES), I32),
            pltpu.VMEM((RING, OWN, LANES), I32),
            pltpu.VMEM((IN_SLOT, LANES), F32),
            pltpu.VMEM((RING, IN_SLOT, LANES), BF16),
            pltpu.VMEM((RING, IN_SLOT, LANES), BF16),
            pltpu.VMEM((OWN, PADDED, LANES), F32),
            pltpu.VMEM((OWN, PADDED, LANES), F32),
            pltpu.VMEM((PADDED, 2 * LANES), BF16),
            pltpu.VMEM((OWN, PADDED, 2 * LANES), BF16),
            pltpu.VMEM((PADDED, 2 * LANES), BF16),
            pltpu.VMEM((2 * SLOT, LANES), F32),
            pltpu.VMEM((PADDED, LANES), F32),
            pltpu.VMEM((PEERS, SLOT, LANES), F32),
            pltpu.VMEM((PEERS, SLOT, LANES), F32),
            pltpu.VMEM((SLOT, LANES), F32),
            pltpu.VMEM((DEPTH, SLOT, LANES), F32),
            pltpu.VMEM((SLOT, LANES), BF16),
            pltpu.VMEM((PEERS, SLOT, LANES), BF16),
            pltpu.VMEM((PADDED, LANES), F32),
            pltpu.VMEM((OWN, PADDED, LANES), F32),
            pltpu.VMEM((OWN, PADDED, LANES), F32),
            pltpu.VMEM((OUT_SLOT, LANES), F32),
            pltpu.VMEM((RING, OUT_SLOT, LANES), BF16),
            pltpu.VMEM((RING, OUT_SLOT, LANES), BF16),
            dma((RING,)), dma((RING,)), dma((RING,)), dma((RING,)), dma((RING,)), dma((RING,)),
            dma((PEERS,)), dma((PEERS,)), dma((DEPTH,)), dma((DEPTH,)), dma((PEERS,)), dma((PEERS,)),
            dma((RING,)), dma((RING,)),
        ],
        compiler_params=pltpu.CompilerParams(collective_id=0, has_side_effects=True),
    )(amplitudes, integrals, fock_block, irrep, virtual_energy.reshape(1, NV), pair_irrep, pair_energy)

    step = 2
    return pl.pallas_call(
        expand_kernel,
        name="expand",
        grid=(RING // step,),
        out_shape=jax.ShapeDtypeStruct((GROUP_PAIRS, ROWS, NV), F32),
        in_specs=[
            pl.BlockSpec((step, OUT_SLOT, LANES), lambda j: (j, 0, 0)),
            pl.BlockSpec((step, OWN, LANES), lambda j: (j, 0, 0)),
            pl.BlockSpec((OUT_HALF, LANES), lambda j: (0, 0)),
            pl.BlockSpec((1, NV), lambda j: (0, 0)),
        ],
        out_specs=pl.BlockSpec((step * OWN, ROWS, NV), lambda j: (j, 0, 0)),
    )(result, irreps, row_key, irrep)


def solution(mesh):
    in_specs = (
        P("grp", "ing", None),
        P("grp", "ing", None),
        P("ing", None),
        P(),
        P(("grp", "ing")),
        P(("grp", "ing")),
        P(),
    )
    out_specs = P("grp", "ing", None)
    return jax.shard_map(body, mesh=mesh, in_specs=in_specs, out_specs=out_specs, check_vma=False)
```

time: 517 us -> 84.7 us (0.16)
  waiting for transfers between devices: 342 us -> 0 us
  blocking collectives: 72.8 us -> 0 us
  Pallas kernels: 0 us -> 67.8 us
  local copies, waits for them, and re-layouts: 45.7 us -> 16.3 us
  between operations: 14.9 us -> 0.01 us
  other arithmetic: 14.3 us -> 0 us
  matrix products: 12.9 us -> 0 us
  starting transfers between devices: 12.2 us -> 0 us
    psum x1 -> x0, waiting for transfers between devices: 252 us -> none  [body(): correction = lax.psum(partial_value, ('grp', 'ing'))]
    all_to_all x2 -> x0, waiting for transfers between devices: 81.5 us -> none  [the longest x1 43.1 us: body(): lax.all_to_all(amplitudes, 'ing', split_axis=0, concat_axis=1, tiled=True)]
    all_to_all x1 -> x0, blocking collectives: 72.8 us -> none  [body(): lax.all_to_all(scaled, 'ing', split_axis=1, concat_axis=0, tiled=True)]
    pallas_call x0 -> x2, Pallas kernels: none -> 67.8 us  [the longest x1 62.1 us: body(): pl.pallas_call(main_kernel, name='residual', out_shape=(jax.ShapeDtypeStr...]
    all_to_all x4 -> x0, local copies, waits for them, and re-layouts: 21.6 us -> none  [the longest x2 13.5 us: body(): lax.all_to_all(scaled, 'ing', split_axis=1, concat_axis=0, tiled=True)]
    dot_general x2 -> x0, matrix products: 12.9 us -> none  [the longest x1 8.05 us: body(): jnp.einsum('pae,be->pab', amp_masked, operator_vv, preferred_element_type...]
    all_to_all x2 -> x0, starting transfers between devices: 12.1 us -> none  [the longest x1 7.58 us: body(): lax.all_to_all(amplitudes, 'ing', split_axis=0, concat_axis=1, tiled=True)]
    all_gather x1 -> x0, waiting for transfers between devices: 8.07 us -> none  [body(): fock_full = lax.all_gather(fock_block, 'ing', axis=0, tiled=True)]
  transfers between devices with their start and end apart: 4 -> 0, of which waited for: 4 -> 0; matrix products, arithmetic and copies ran while one was open for 6% -> 0% of each run, Pallas kernels for 0% -> 0%
where the time goes in v1:
time: 84.7 us; the launch traced here: 84.1 us
  Pallas kernels  67.8 us (80%)
  local copies, waits for them, and re-layouts  16.3 us (19%)
    pallas_call x1, Pallas kernels, body(): pl.pallas_call(main_kernel, name='residual', out_shape=(jax.ShapeDtypeStr...  62.1 us
    unnamed x4, local copies, waits for them, and re-layouts  7.12 us
    pallas_call x1, local copies, waits for them, and re-layouts, body(): pl.pallas_call(expand_kernel, name='expand', grid=(RING // step,), out_sh...  6.45 us
    pallas_call x1, Pallas kernels, body(): pl.pallas_call(expand_kernel, name='expand', grid=(RING // step,), out_sh...  5.75 us

profile of v1, /device:TPU:1, one launch (start us, length us, event | category | flops | bytes accessed | tf_op | source)
XLA Modules:
  0.0 84.1 jit_solution(17599702113799700961)
XLA Ops:
  0.0 0.0 copy-start
  0.0 1.4 %reshape.6.irrep = s32[1,800]{1,0:T(1,128)} reshape(s32[800]{0:T(1024)} %param.10) | data formatting | bytes 6400 | tf_op jit(solution)/shard_map/reshape | solution.py:404
  1.4 1.3 %reshape.7.energy = f32[1,800]{1,0:T(1,128)} reshape(f32[800]{0:T(1024)} %param.13) | data formatting | bytes 6400 | tf_op jit(solution)/shard_map/reshape | solution.py:453
  2.7 4.5 %copy.8.amps = bf16[32,50,800]{2,1,0:T(8,128)(2,1)} copy(bf16[32,50,800]{2,0,1:T(8,128)(2,1)} %param.7) | data formatting | bytes 5120000 | tf_op args[0]
  7.2 0.0 copy-done
  7.2 2.6 %copy.9.ints = bf16[32,50,800]{2,1,0:T(8,128)(2,1)} copy(bf16[32,50,800]{2,0,1:T(8,128)(2,1)S(1)} %copy-done) | data formatting | bytes 5120000 | tf_op args[1]
  9.8 62.1 %residual.1 = (bf16[16,112,128]{2,1,0:T(8,128)(2,1)}, s32[16,2,128]{2,1,0:T(2,128)}, s32[56,128]{1,0:T(8,128)}) custom-call(bf16[32,50,800]{2,1,0:T(8,128)(2,1)} %copy.8.amps, bf16[32,50,800]{2,1,0:T(8,128)(2,1)} %copy.9.ints, bf16[50,800]{1,0:T(8,128)(2,1)} %fock.1, s32[1,800]{1,0:T(1,128)} %reshape.6.irrep, f32[1,800]{1,0:T(1,128)} %reshape.7.energy, ...), custom_call_target="tpu_custom_call" | custom-call | tf_op jit(solution)/shard_map/residual/pallas_call | solution.py:406
  71.9 5.8 %expand.1 = f32[32,50,800]{2,1,0:T(8,128)} custom-call(bf16[16,112,128]{2,1,0:T(8,128)(2,1)} %get-tuple-element.8.folded, s32[16,2,128]{2,1,0:T(2,128)} %get-tuple-element.9.irreps, s32[56,128]{1,0:T(8,128)} %get-tuple-element.10.row_key, s32[1,800]{1,0:T(1,128)} %reshape.6.irrep), custom_call_target="tpu_custom_call" | custom-call | tf_op jit(solution)/shard_map/expand/pallas_call | solution.py:456
  77.7 6.4 %copy.10 = f32[32,50,800]{2,0,1:T(8,128)} copy(f32[32,50,800]{2,1,0:T(8,128)} %expand.1) | data formatting | bytes 10240000 | tf_op jit(solution)/shard_map/expand/pallas_call | solution.py:456
Async XLA Ops:
  0.0 7.2 %copy-start = (bf16[32,50,800]{2,0,1:T(8,128)(2,1)S(1)}, bf16[32,50,800]{2,0,1:T(8,128)(2,1)}, u32[]{:S(2)}) copy-start(bf16[32,50,800]{2,0,1:T(8,128)(2,1)} %param.8) | copy-start | bytes 7680004

commit v2 on v1

--- a/solution.py
+++ b/solution.py
@@ -10,6 +10,7 @@
 NV, LANES, TILES = 800, 128, 7
 PADDED = LANES * TILES
 ROWS, OWN, GROUP_PAIRS = 50, 2, 32
+GROUP = 8
 RING, DEPTH, SIDE = 16, 8, 4
 PEERS = 2 * RING
 SLICE, SLOT = 25, 32
@@ -29,8 +30,8 @@
 
 def main_kernel(
     amps, ints, fock, irrep, energy, pair_irrep, pair_energy,
-    result, irreps_out, row_key_out,
-    amp_in, int_in, col_key, col_energy, row_key, row_energy, own_key,
+    result, pair_key_out, own_wide_out, col_wide_out,
+    amp_in, int_in, col_key, col_energy, row_key, row_energy, own_key, pair_key, fold_a, fold_b,
     g_send, g_recv, stage, pack_send, pack_recv, nat_a, nat_b, lhs, rhs, int_rhs,
     fock_fold, corr, red_send, red_recv, z_send, z_recv, op_send, op_recv, op_nat,
     inverse, scaled, out_stage, out_send, out_recv,
@@ -51,15 +52,15 @@
     def on_plane(i, c):
         return (z * 2 + c, i)
 
-    def chunk(j):
-        place = pl.ds(OWN * j, OWN)
+    def chunk(h):
+        place = pl.ds(GROUP * h, GROUP)
         return (
-            pltpu.make_async_copy(amps.at[place], amp_in.at[place], amp_sem.at[j]),
-            pltpu.make_async_copy(ints.at[place], int_in.at[place], int_sem.at[j]),
+            pltpu.make_async_copy(amps.at[:, place], amp_in.at[h], amp_sem.at[h]),
+            pltpu.make_async_copy(ints.at[:, place], int_in.at[h], int_sem.at[h]),
         )
 
     def load(k, carry):
-        for copy in chunk(plane_peer(k)):
+        for copy in chunk((y + k) % SIDE):
             copy.start()
         return carry
 
@@ -79,7 +80,7 @@
 
     lax.fori_loop(1, PEERS, greet, 0)
     lax.fori_loop(1, DEPTH, greet_z, 0)
-    lax.fori_loop(0, RING, load, 0)
+    lax.fori_loop(0, SIDE, load, 0)
 
     for q in range(OWN):
         g_send[q : q + 1, :] = jnp.full((1, LANES), pair_irrep[q], I32)
@@ -87,18 +88,21 @@
 
     for t in range(TILES):
         if t < TILES - 1:
-            col_key[t : t + 1, :] = irrep[:, LANES * t : LANES * (t + 1)]
+            col_key[t : t + 1, :] = irrep[LANES * t : LANES * (t + 1)].reshape(1, LANES)
+            col_energy[t : t + 1, :] = energy[LANES * t : LANES * (t + 1)].reshape(1, LANES)
         else:
-            col_key[t : t + 1, :] = jnp.concatenate(
-                [irrep[:, LANES * t : NV], jnp.full((1, PADDED - NV), -1, I32)], axis=1
-            )
-        col_energy[t : t + 1, :] = tile_of(energy[...], t)
+            col_key[t : t + 1, :] = jnp.full((1, LANES), -1, I32)
+            col_key[t : t + 1, 0 : NV - LANES * t] = irrep[LANES * t : NV].reshape(1, NV - LANES * t)
+            col_energy[t : t + 1, :] = jnp.zeros((1, LANES), F32)
+            col_energy[t : t + 1, 0 : NV - LANES * t] = energy[LANES * t : NV].reshape(1, NV - LANES * t)
+        col_wide_out[8 * t : 8 * (t + 1), :] = jnp.broadcast_to(col_key[t : t + 1, :], (8, LANES))
     for t in range(TILES):
         place = slice(LANES * t, LANES * (t + 1))
         keys = jnp.broadcast_to(col_key[t : t + 1, :].astype(F32), (LANES, LANES))
         row_key[place, :] = keys.T.astype(I32)
     own_key[...] = row_key[pl.ds(ROWS * ing, OUT_HALF), :]
-    row_key_out[...] = own_key[...]
+    for a in range(ROWS):
+        own_wide_out[8 * a : 8 * (a + 1), :] = jnp.broadcast_to(own_key[a : a + 1, :], (8, LANES))
 
     pl.semaphore_wait(barrier, PEERS - 1 + DEPTH - 1)
 
@@ -120,38 +124,65 @@
             recv_sem=p_rsem.at[slot], device_id=on_plane(i, core), device_id_type=MESH,
         )
 
-    def fold_chunk(j):
-        keys = own_key[0:ROWS, :]
-        for q in range(OWN):
-            wanted = keys ^ g_recv[j, q : q + 1, :]
-            for which, source in ((0, amp_in), (1, int_in)):
-                folded = jnp.zeros((ROWS, LANES), F32)
-                for t in range(TILES):
-                    if t < TILES - 1:
-                        part = source[OWN * j + q, :, LANES * t : LANES * (t + 1)].astype(F32)
-                    else:
-                        part = source[OWN * j + q, :, LANES * t : NV].astype(F32)
-                        part = jnp.concatenate([part, jnp.zeros((ROWS, PADDED - NV), F32)], axis=1)
-                    folded = jnp.where(wanted == col_key[t : t + 1, :], part, folded)
-                first = ROWS * (which * OWN + q)
-                stage[first : first + ROWS, :] = folded
-        return stage[...].astype(BF16)
+    def fold_rows(h):
+        pairs = pair_key[pl.ds(pl.multiple_of(GROUP * h, GROUP), GROUP), :]
+
+        def some_rows(b, carry):
+            for a in range(ROWS // 10):
+                row = b * (ROWS // 10) + a
+                place = pl.ds(pl.multiple_of(GROUP * row, GROUP), GROUP)
+                wanted = own_wide_out[place, :] ^ pairs
+                for source, folds in ((amp_in, fold_a), (int_in, fold_b)):
+                    folded = jnp.zeros((GROUP, LANES), F32)
+                    for t in range(TILES):
+                        part = tile_of(source[h, row], t).astype(F32)
+                        folded = jnp.where(wanted == col_wide_out[8 * t : 8 * (t + 1), :], part, folded)
+                    folds[place, :] = folded
+            return carry
+
+        lax.fori_loop(0, 10, some_rows, 0)
 
     stage[4 * ROWS : IN_SLOT, :] = jnp.zeros((IN_SLOT - 4 * ROWS, LANES), F32)
 
     def pack_step(k, carry):
-        j = plane_peer(k)
-        g_copy(ing, j).wait_recv()
-        for copy in chunk(j):
+        h = (y + k) % SIDE
+        for i in range(SIDE):
+            j = SIDE * h + i
+
+            @pl.when(j != ing)
+            def _():
+                g_copy(ing, j).wait_recv()
+
+            pair_key[pl.ds(OWN * j, OWN), :] = g_recv[j]
+        for copy in chunk(h):
             copy.wait()
-        pack_send[j] = fold_chunk(j)
-        pack_copy(j, ing).start()
-        return carry
-
-    lax.fori_loop(1, RING, pack_step, 0)
-    for copy in chunk(ing):
-        copy.wait()
-    pack_recv[ing] = fold_chunk(ing)
+        fold_rows(h)
+
+        def pack_one(i, inner):
+            place = (x + i) % SIDE
+            j = SIDE * h + place
+            for q in range(OWN):
+                for which, folds in ((0, fold_a), (1, fold_b)):
+                    first = ROWS * (which * OWN + q)
+                    stage[first : first + ROWS, :] = folds[pl.ds(OWN * place + q, ROWS, stride=GROUP), :]
+            packed = stage[...].astype(BF16)
+
+            @pl.when(j != ing)
+            def _():
+                pack_send[j] = packed
+                pack_copy(j, ing).start()
+
+            @pl.when(j == ing)
+            def _():
+                pack_recv[j] = packed
+
+            return inner
+
+        lax.fori_loop(0, SIDE, pack_one, 0)
+        return carry
+
+    lax.fori_loop(0, SIDE, pack_step, 0)
+    pair_key_out[...] = pair_key[...]
 
     fock_rows = fock[...].astype(F32)
     fock_keys = own_key[0:ROWS, :]
@@ -348,7 +379,6 @@
 
     lax.fori_loop(0, RING, out_step, 0)
     out_recv[ing] = out_rows(ing)
-    irreps_out[...] = g_recv[...]
 
     def sent(k, carry):
         i = plane_peer(k)
@@ -372,55 +402,63 @@
 
     lax.fori_loop(1, DEPTH, sent_z, 0)
 
+    def spread(j):
+        values = out_recv[j].astype(F32)
+        for q in range(OWN):
+            rows = values[OUT_HALF * q : OUT_HALF * q + ROWS, :]
+            result[pl.ds(OWN * j + q, ROWS, stride=GROUP_PAIRS), :] = rows
+
+    spread(ing)
+
     def out_wait(k, carry):
-        j = plane_peer(k)
+        j = plane_peer(RING - k)
         out_copy(ing, j).wait_recv()
+        spread(j)
         out_copy(j, ing).wait_send()
         return carry
 
     lax.fori_loop(1, RING, out_wait, 0)
-    result[...] = out_recv[...]
-
-
-def expand_kernel(folded, irreps, row_key, irrep, update):
-    keys = row_key[0:ROWS, :]
-    for b in range(folded.shape[0]):
-        values = folded[b].astype(F32)
-        for q in range(OWN):
-            part = values[OUT_HALF * q : OUT_HALF * q + ROWS, :]
-            wanted = keys ^ irreps[b, q : q + 1, :]
+
+
+def expand_kernel(folded, pair_key, own_wide, col_wide, update):
+    for a in range(update.shape[0]):
+        for s in range(GROUP_PAIRS // GROUP):
+            pairs = slice(GROUP * s, GROUP * (s + 1))
+            wanted = pair_key[pairs, :] ^ own_wide[8 * a : 8 * (a + 1), :]
+            values = folded[GROUP_PAIRS * a + GROUP * s : GROUP_PAIRS * a + GROUP * (s + 1), :]
             for t in range(TILES):
                 width = min(LANES, NV - LANES * t)
-                cols = slice(LANES * t, LANES * t + width)
-                update[OWN * b + q, :, cols] = jnp.where(
-                    wanted[:, 0:width] == irrep[:, cols], part[:, 0:width], 0.0
-                )
+                kept = jnp.where(wanted == col_wide[8 * t : 8 * (t + 1), :], values, 0.0)
+                update[a, pairs, LANES * t : LANES * t + width] = kept[:, 0:width]
 
 
 def body(amplitudes, integrals, fock_block, virtual_irrep, pair_irrep, pair_energy, virtual_energy):
     vmem = pl.BlockSpec(memory_space=pltpu.VMEM)
     smem = pl.BlockSpec(memory_space=pltpu.SMEM)
     hbm = pl.BlockSpec(memory_space=pl.ANY)
-    irrep = virtual_irrep.reshape(1, NV)
     dma = pltpu.SemaphoreType.DMA
-    result, irreps, row_key = pl.pallas_call(
+    result, pair_key, own_wide, col_wide = pl.pallas_call(
         main_kernel,
         name="residual",
         out_shape=(
-            jax.ShapeDtypeStruct((RING, OUT_SLOT, LANES), BF16),
-            jax.ShapeDtypeStruct((RING, OWN, LANES), I32),
-            jax.ShapeDtypeStruct((OUT_HALF, LANES), I32),
+            jax.ShapeDtypeStruct((ROWS * GROUP_PAIRS, LANES), F32),
+            jax.ShapeDtypeStruct((GROUP_PAIRS, LANES), I32),
+            jax.ShapeDtypeStruct((ROWS * 8, LANES), I32),
+            jax.ShapeDtypeStruct((TILES * 8, LANES), I32),
         ),
         in_specs=[hbm, hbm, vmem, vmem, vmem, smem, smem],
-        out_specs=(vmem, vmem, vmem),
+        out_specs=(vmem, vmem, vmem, vmem),
         scratch_shapes=[
-            pltpu.VMEM((GROUP_PAIRS, ROWS, NV), BF16),
-            pltpu.VMEM((GROUP_PAIRS, ROWS, NV), BF16),
+            pltpu.VMEM((GROUP_PAIRS // GROUP, ROWS, GROUP, NV), BF16),
+            pltpu.VMEM((GROUP_PAIRS // GROUP, ROWS, GROUP, NV), BF16),
             pltpu.VMEM((8, LANES), I32),
             pltpu.VMEM((8, LANES), F32),
             pltpu.VMEM((PADDED, LANES), I32),
             pltpu.VMEM((PADDED, LANES), F32),
             pltpu.VMEM((OUT_HALF, LANES), I32),
+            pltpu.VMEM((GROUP_PAIRS, LANES), I32),
+            pltpu.VMEM((ROWS * GROUP, LANES), F32),
+            pltpu.VMEM((ROWS * GROUP, LANES), F32),
             pltpu.VMEM((OWN, LANES), I32),
             pltpu.VMEM((RING, OWN, LANES), I32),
             pltpu.VMEM((IN_SLOT, LANES), F32),
@@ -445,27 +483,31 @@
             pltpu.VMEM((OUT_SLOT, LANES), F32),
             pltpu.VMEM((RING, OUT_SLOT, LANES), BF16),
             pltpu.VMEM((RING, OUT_SLOT, LANES), BF16),
-            dma((RING,)), dma((RING,)), dma((RING,)), dma((RING,)), dma((RING,)), dma((RING,)),
+            dma((SIDE,)), dma((SIDE,)), dma((RING,)), dma((RING,)), dma((RING,)), dma((RING,)),
             dma((PEERS,)), dma((PEERS,)), dma((DEPTH,)), dma((DEPTH,)), dma((PEERS,)), dma((PEERS,)),
             dma((RING,)), dma((RING,)),
         ],
         compiler_params=pltpu.CompilerParams(collective_id=0, has_side_effects=True),
-    )(amplitudes, integrals, fock_block, irrep, virtual_energy.reshape(1, NV), pair_irrep, pair_energy)
-
-    step = 2
-    return pl.pallas_call(
+    )(
+        jnp.transpose(amplitudes, (1, 0, 2)), jnp.transpose(integrals, (1, 0, 2)), fock_block,
+        virtual_irrep, virtual_energy, pair_irrep, pair_energy,
+    )
+
+    step = 25
+    update = pl.pallas_call(
         expand_kernel,
         name="expand",
-        grid=(RING // step,),
-        out_shape=jax.ShapeDtypeStruct((GROUP_PAIRS, ROWS, NV), F32),
+        grid=(ROWS // step,),
+        out_shape=jax.ShapeDtypeStruct((ROWS, GROUP_PAIRS, NV), F32),
         in_specs=[
-            pl.BlockSpec((step, OUT_SLOT, LANES), lambda j: (j, 0, 0)),
-            pl.BlockSpec((step, OWN, LANES), lambda j: (j, 0, 0)),
-            pl.BlockSpec((OUT_HALF, LANES), lambda j: (0, 0)),
-            pl.BlockSpec((1, NV), lambda j: (0, 0)),
+            pl.BlockSpec((step * GROUP_PAIRS, LANES), lambda j: (j, 0)),
+            pl.BlockSpec((GROUP_PAIRS, LANES), lambda j: (0, 0)),
+            pl.BlockSpec((step * 8, LANES), lambda j: (j, 0)),
+            pl.BlockSpec((TILES * 8, LANES), lambda j: (0, 0)),
         ],
-        out_specs=pl.BlockSpec((step * OWN, ROWS, NV), lambda j: (j, 0, 0)),
-    )(result, irreps, row_key, irrep)
+        out_specs=pl.BlockSpec((step, GROUP_PAIRS, NV), lambda j: (j, 0, 0)),
+    )(result, pair_key, own_wide, col_wide)
+    return jnp.transpose(update, (1, 0, 2))
 
 
 def solution(mesh):

time: 84.7 us -> 66.5 us (0.79)
  local copies, waits for them, and re-layouts: 16.3 us -> 0 us
  Pallas kernels: 67.8 us -> 66.3 us
    unnamed x4 -> x0, local copies, waits for them, and re-layouts: 7.12 us -> none
    pallas_call x1 -> x0, local copies, waits for them, and re-layouts: 6.45 us -> none  [body(): pl.pallas_call(expand_kernel, name='expand', grid=(RING // step,), out_sh...]
    reshape x2 -> x0, local copies, waits for them, and re-layouts: 2.71 us -> none  [the longest x1 1.43 us: body(): irrep = virtual_irrep.reshape(1, NV)]
    pallas_call x1, Pallas kernels: 5.75 us -> 3.76 us  [body(): pl.pallas_call(expand_kernel, name='expand', grid=(ROWS // step,), out_sh...]
where the time goes in v2:
time: 66.5 us; the launch traced here: 66.3 us
  Pallas kernels  66.3 us (100%)
    pallas_call x1, Pallas kernels, body(): pl.pallas_call(main_kernel, name='residual', out_shape=(jax.ShapeDtypeStr...  62.6 us
    pallas_call x1, Pallas kernels, body(): pl.pallas_call(expand_kernel, name='expand', grid=(ROWS // step,), out_sh...  3.76 us

profile of v2, /device:TPU:1, one launch (start us, length us, event | category | flops | bytes accessed | tf_op | source)
XLA Modules:
  0.0 66.3 jit_solution(12219199806301240923)
XLA Ops:
  0.0 62.6 %residual.1 = (f32[1600,128]{1,0:T(8,128)}, s32[32,128]{1,0:T(8,128)}, s32[400,128]{1,0:T(8,128)}, s32[56,128]{1,0:T(8,128)}) custom-call(bf16[50,32,800]{2,1,0:T(8,128)(2,1)} %bitcast.3, bf16[50,32,800]{2,1,0:T(8,128)(2,1)} %bitcast.4, bf16[50,800]{1,0:T(8,128)(2,1)} %fock.1, s32[800]{0:T(1024)} %irrep.1, f32[800]{0:T(1024)} %energy.1, s32[2]{0:T(128)} %pair_irrep.1, ...), custom_call_target="tpu_custom_call" | custom-call | tf_op jit(solution)/shard_map/residual/pallas_call | solution.py:440
  62.6 3.8 %expand.1 = f32[50,32,800]{2,1,0:T(8,128)} custom-call(f32[1600,128]{1,0:T(8,128)} %get-tuple-element.9.folded, s32[32,128]{1,0:T(8,128)} %get-tuple-element.10.pair_key, s32[400,128]{1,0:T(8,128)} %get-tuple-element.11.own_wide, s32[56,128]{1,0:T(8,128)} %get-tuple-element.12.col_wide), custom_call_target="tpu_custom_call" | custom-call | tf_op jit(solution)/shard_map/expand/pallas_call | solution.py:497

commit v3 on v2

v3 whole, which is shorter than its diff:
```python
import functools

import jax
import jax.numpy as jnp
from jax import lax
from jax.experimental import pallas as pl
from jax.experimental.pallas import tpu as pltpu
from jax.sharding import PartitionSpec as P

NV, LANES, TILES = 800, 128, 7
PADDED = LANES * TILES
ROWS, OWN, GROUP_PAIRS = 50, 2, 32
GROUP = 16
HALVES = GROUP_PAIRS // GROUP
RING, DEPTH, SIDE = 16, 8, 4
PEERS = 2 * RING
SLICE, SLOT = 26, 32
WIDE = 56
MESH = pl.DeviceIdType.MESH
F32, BF16, I32 = jnp.float32, jnp.bfloat16, jnp.int32
NT = (((1,), (1,)), ((), ()))


def tile_of(array, t):
    if t < TILES - 1:
        return array[:, LANES * t : LANES * (t + 1)]
    last = array[:, LANES * t : NV]
    pad = jnp.zeros((array.shape[0], PADDED - NV), array.dtype)
    return jnp.concatenate([last, pad], axis=1)


def main_kernel(
    amps, ints, fock, irrep, energy, pair_irrep, pair_energy,
    result, pair_key_out, own_wide_out, col_wide_out,
    amp_in, int_in, col_key, col_half, col_energy, row_key, row_energy, own_key, pair_key,
    g_send, g_recv, fold, pack_recv, mixed, lhs, rhs, int_rhs,
    fock_fold, corr, red_recv, z_send, z_recv, op_send, op_all,
    inverse, out_send, out_recv,
    amp_sem, int_sem, g_ssem, g_rsem, p_ssem, p_rsem, r_ssem, r_rsem,
    z_ssem, z_rsem, o_ssem, o_rsem, t_ssem, t_rsem, own_sem,
):
    grp, ing = lax.axis_index("grp"), lax.axis_index("ing")
    z, core = grp // 2, grp % 2
    y, x = ing // SIDE, ing % SIDE
    me = ing * 2 + core

    def plane_peer(k):
        return ((y + k // SIDE) % SIDE) * SIDE + (x + k % SIDE) % SIDE

    def far_peer(k):
        return ((y + 2 + k // SIDE) % SIDE) * SIDE + (x + 2 + k % SIDE) % SIDE

    def on_plane(i, c):
        return (z * 2 + c, i)

    def chunk(h):
        place = pl.ds(GROUP * h, GROUP)
        return (
            pltpu.make_async_copy(amps.at[:, place], amp_in.at[h], amp_sem.at[h]),
            pltpu.make_async_copy(ints.at[:, place], int_in.at[h], int_sem.at[h]),
        )

    def load(k, carry):
        for copy in chunk((y // 2 + k) % HALVES):
            copy.start()
        return carry

    barrier = pltpu.get_barrier_semaphore()

    def greet(k, carry):
        pl.semaphore_signal(
            barrier, inc=1, device_id=on_plane(plane_peer(k // 2), (core + k) % 2), device_id_type=MESH
        )
        return carry

    def greet_z(k, carry):
        pl.semaphore_signal(
            barrier, inc=1, device_id=(((z + k) % DEPTH) * 2 + core, ing), device_id_type=MESH
        )
        return carry

    lax.fori_loop(1, PEERS, greet, 0)
    lax.fori_loop(1, DEPTH, greet_z, 0)
    lax.fori_loop(0, HALVES, load, 0)

    for q in range(OWN):
        g_send[q : q + 1, :] = jnp.full((1, LANES), pair_irrep[q], I32)
    g_recv[ing] = g_send[...]

    pl.semaphore_wait(barrier, PEERS - 1 + DEPTH - 1)

    def g_copy(i, slot, c=None):
        return pltpu.make_async_remote_copy(
            src_ref=g_send, dst_ref=g_recv.at[slot], send_sem=g_ssem.at[i], recv_sem=g_rsem.at[slot],
            device_id=on_plane(i, core), device_id_type=MESH,
        )

    def g_start(k, carry):
        g_copy(plane_peer(k), ing).start()
        return carry

    lax.fori_loop(1, RING, g_start, 0)

    for t in range(TILES):
        if t < TILES - 1:
            col_key[t : t + 1, :] = irrep[LANES * t : LANES * (t + 1)].reshape(1, LANES)
            col_energy[t : t + 1, :] = energy[LANES * t : LANES * (t + 1)].reshape(1, LANES)
        else:
            col_key[t : t + 1, :] = jnp.full((1, LANES), -1, I32)
            col_key[t : t + 1, 0 : NV - LANES * t] = irrep[LANES * t : NV].reshape(1, NV - LANES * t)
            col_energy[t : t + 1, :] = jnp.zeros((1, LANES), F32)
            col_energy[t : t + 1, 0 : NV - LANES * t] = energy[LANES * t : NV].reshape(1, NV - LANES * t)
        col_wide_out[8 * t : 8 * (t + 1), :] = jnp.broadcast_to(col_key[t : t + 1, :], (8, LANES))
        col_half[GROUP * t : GROUP * (t + 1), :] = jnp.broadcast_to(
            col_key[t : t + 1, :].astype(F32), (GROUP, LANES)
        ).astype(BF16)
    for t in range(TILES):
        place = slice(LANES * t, LANES * (t + 1))
        keys = jnp.broadcast_to(col_key[t : t + 1, :].astype(F32), (LANES, LANES))
        row_key[place, :] = keys.T.astype(I32)
    own_key[...] = row_key[pl.ds(ROWS * ing, WIDE), :]
    for a in range(ROWS):
        own_wide_out[8 * a : 8 * (a + 1), :] = jnp.broadcast_to(own_key[a : a + 1, :], (8, LANES))

    def pack_copy(i, slot):
        return pltpu.make_async_remote_copy(
            src_ref=fold.at[:, :, pl.ds(OWN * i, OWN), :], dst_ref=pack_recv.at[:, pl.ds(ROWS * slot, ROWS)],
            send_sem=p_ssem.at[i], recv_sem=p_rsem.at[slot], device_id=on_plane(i, core),
            device_id_type=MESH,
        )

    def fold_rows(h):
        pairs = pair_key[pl.ds(pl.multiple_of(GROUP * h, GROUP), GROUP), :]
        place = pl.ds(pl.multiple_of(GROUP * h, GROUP), GROUP)

        def some_rows(b, carry):
            for a in range(ROWS // 10):
                row = b * (ROWS // 10) + a
                key = own_wide_out[pl.ds(pl.multiple_of(8 * row, 8), 8), :]
                wanted = (jnp.concatenate([key, key], axis=0) ^ pairs).astype(F32).astype(BF16)
                for which, source in ((0, amp_in), (1, int_in)):
                    folded = jnp.zeros((GROUP, LANES), BF16)
                    for t in range(TILES):
                        part = tile_of(source[h, row], t)
                        folded = jnp.where(wanted == col_half[GROUP * t : GROUP * (t + 1), :], part, folded)
                    fold[which, row, place, :] = folded
            return carry

        lax.fori_loop(0, 10, some_rows, 0)

    own_rows = pltpu.make_async_copy(
        fold.at[:, :, pl.ds(OWN * ing, OWN), :], pack_recv.at[:, pl.ds(ROWS * ing, ROWS)], own_sem.at[0]
    )

    def pack_step(k, carry):
        h = (y // 2 + k) % HALVES
        for i in range(RING // HALVES):
            j = RING // HALVES * h + i

            @pl.when(j != ing)
            def _():
                g_copy(ing, j).wait_recv()

            pair_key[pl.ds(OWN * j, OWN), :] = g_recv[j]
        for copy in chunk(h):
            copy.wait()
        fold_rows(h)
        for i in range(RING // HALVES):
            j = RING // HALVES * h + i

            @pl.when(j != ing)
            def _():
                pack_copy(j, ing).start()

            @pl.when(j == ing)
            def _():
                own_rows.start()

        return carry

    lax.fori_loop(0, HALVES, pack_step, 0)
    pair_key_out[...] = pair_key[...]

    fock_rows = fock[...].astype(F32)
    fock_keys = own_key[0:ROWS, :]
    folded_fock = jnp.zeros((ROWS, LANES), F32)
    for t in range(TILES):
        folded_fock = jnp.where(fock_keys == col_key[t : t + 1, :], tile_of(fock_rows, t), folded_fock)
    fock_fold[...] = jnp.zeros(fock_fold.shape, F32)
    fock_fold[0:ROWS, :] = folded_fock
    for t in range(TILES):
        place = slice(LANES * t, LANES * (t + 1))
        row_energy[place, :] = jnp.broadcast_to(col_energy[t : t + 1, :], (LANES, LANES)).T
    for q in range(OWN):
        for t in range(TILES):
            place = slice(LANES * t, LANES * (t + 1))
            wanted = row_key[place, :] ^ pair_irrep[q]
            other = jnp.zeros((LANES, LANES), F32)
            for u in range(TILES):
                other = jnp.where(wanted == col_key[u : u + 1, :], col_energy[u : u + 1, :], other)
            inverse[q, place, :] = 1.0 / (pair_energy[q] - row_energy[place, :] - other)
    lhs[NV:PADDED, :] = jnp.zeros((PADDED - NV, 2 * LANES), BF16)
    int_rhs[NV:PADDED, :] = jnp.zeros((PADDED - NV, 2 * LANES), BF16)
    rhs[:, NV:PADDED, :] = jnp.zeros((OWN, PADDED - NV, 2 * LANES), BF16)

    own_rows.wait()

    def pack_wait(k, carry):
        pack_copy(ing, plane_peer(RING - k)).wait_recv()
        return carry

    lax.fori_loop(1, RING, pack_wait, 0)
    for which, target in ((0, lhs), (1, int_rhs)):
        mixed[...] = pack_recv[which].reshape(OWN * NV, LANES).astype(F32)
        for q in range(OWN):
            target[0:NV, LANES * q : LANES * (q + 1)] = mixed[pl.ds(q, NV, stride=OWN), :].astype(BF16)

    for r in range(TILES):
        place = slice(LANES * r, LANES * (r + 1))
        low, high = max(r - 1, 0), min(r + 2, TILES)
        block = lax.dot_general(
            lhs[place, :], int_rhs[LANES * low : LANES * high, :], NT, preferred_element_type=F32
        )
        keys = row_key[place, :]
        folded = jnp.zeros((LANES, LANES), F32)
        for t in range(low, high):
            part = block[:, LANES * (t - low) : LANES * (t - low + 1)]
            folded = jnp.where(keys == col_key[t : t + 1, :], part, folded)
        corr[place, :] = folded

    def red_copy(i, c, slot):
        return pltpu.make_async_remote_copy(
            src_ref=corr.at[pl.ds(ROWS * i + SLICE * c, SLICE)], dst_ref=red_recv.at[slot, pl.ds(0, SLICE)],
            send_sem=r_ssem.at[i * 2 + c], recv_sem=r_rsem.at[slot], device_id=on_plane(i, c),
            device_id_type=MESH,
        )

    def red_step(k, carry):
        for c in range(2):
            i = far_peer(k)

            @pl.when(i * 2 + c != me)
            def _():
                red_copy(i, c, me).start()

        return carry

    lax.fori_loop(0, RING, red_step, 0)
    red_recv[me, 0:SLICE, :] = corr[pl.ds(ROWS * ing + SLICE * core, SLICE), :]

    for q in range(OWN):
        rhs[q, 0:NV, LANES : 2 * LANES] = -lhs[0:NV, LANES * q : LANES * (q + 1)]

    def red_wait(k, carry):
        i, c = plane_peer(k // 2), (core + k) % 2
        red_copy(ing, core, i * 2 + c).wait_recv()
        return carry

    lax.fori_loop(1, PEERS, red_wait, 0)
    total = red_recv[0, 0:SLICE, :]
    for w in range(1, PEERS):
        total = total + red_recv[w, 0:SLICE, :]
    z_send[0:SLICE, :] = total

    def z_copy(dest, slot):
        return pltpu.make_async_remote_copy(
            src_ref=z_send.at[pl.ds(0, SLICE)], dst_ref=z_recv.at[slot, pl.ds(0, SLICE)], send_sem=z_ssem.at[dest],
            recv_sem=z_rsem.at[slot], device_id=(dest * 2 + core, ing), device_id_type=MESH,
        )

    def z_start(k, carry):
        z_copy((z + 3 + k) % DEPTH, z).start()
        return carry

    lax.fori_loop(1, 5, z_start, 0)
    lax.fori_loop(6, 9, z_start, 0)
    z_recv[z, 0:SLICE, :] = total

    def z_wait(k, carry):
        z_copy(z, (z + k) % DEPTH).wait_recv()
        return carry

    lax.fori_loop(1, DEPTH, z_wait, 0)
    total = z_recv[0, 0:SLICE, :]
    for k in range(1, DEPTH):
        total = total + z_recv[k, 0:SLICE, :]
    op_send[0:SLICE, :] = (fock_fold[pl.ds(SLICE * core, SLICE), :] + total).astype(BF16)

    def op_rows(c):
        return SLICE if c == 0 else ROWS - SLICE

    def op_copy(i, c, source, source_core):
        rows = op_rows(source_core)
        return pltpu.make_async_remote_copy(
            src_ref=op_send.at[pl.ds(0, rows)], dst_ref=op_all.at[pl.ds(ROWS * source + SLICE * source_core, rows)],
            send_sem=o_ssem.at[i * 2 + c], recv_sem=o_rsem.at[source * 2 + source_core],
            device_id=on_plane(i, c), device_id_type=MESH,
        )

    for mine in range(2):

        @pl.when(core == mine)
        def _():
            def op_start(k, carry):
                for c in range(2):
                    i = far_peer(k)

                    @pl.when(i * 2 + c != me)
                    def _():
                        op_copy(i, c, ing, mine).start()

                return carry

            lax.fori_loop(0, RING, op_start, 0)
            own_op = pltpu.make_async_copy(
                op_send.at[pl.ds(0, op_rows(mine))],
                op_all.at[pl.ds(ROWS * ing + SLICE * mine, op_rows(mine))], own_sem.at[1],
            )
            own_op.start()
            own_op.wait()

    def op_wait(k, carry):
        for c in range(2):
            i = plane_peer(k)

            @pl.when(i * 2 + c != me)
            def _():
                op_copy(ing, core, i, c).wait_recv()

        return carry

    lax.fori_loop(0, RING, op_wait, 0)

    operator = op_all[...]
    for q in range(OWN):
        rhs[q, 0:NV, 0:LANES] = operator
        left = jnp.concatenate([lhs[0:NV, LANES * q : LANES * (q + 1)], operator], axis=1)
        keys = row_key[0:NV, :] ^ pair_irrep[q]
        folded = jnp.zeros((NV, LANES), F32)
        for t in range(0, TILES, 2):
            width = min(2, TILES - t)
            block = lax.dot_general(
                left, rhs[q, LANES * t : LANES * (t + width), :], NT, preferred_element_type=F32
            )
            for u in range(width):
                part = block[:, LANES * u : LANES * (u + 1)]
                folded = jnp.where(keys == col_key[t + u : t + u + 1, :], part, folded)
        mixed[pl.ds(q, NV, stride=OWN), :] = folded * inverse[q, 0:NV, :]
    out_send[...] = mixed[...].astype(BF16).reshape(NV, OWN, LANES)

    def out_copy(i, slot):
        return pltpu.make_async_remote_copy(
            src_ref=out_send.at[pl.ds(ROWS * i, ROWS)], dst_ref=out_recv.at[:, pl.ds(OWN * slot, OWN), :],
            send_sem=t_ssem.at[i], recv_sem=t_rsem.at[slot], device_id=on_plane(i, core),
            device_id_type=MESH,
        )

    def out_step(k, carry):
        j = far_peer(k)

        @pl.when(j != ing)
        def _():
            out_copy(j, ing).start()

        return carry

    lax.fori_loop(0, RING, out_step, 0)
    own_out = pltpu.make_async_copy(
        out_send.at[pl.ds(ROWS * ing, ROWS)], out_recv.at[:, pl.ds(OWN * ing, OWN), :], own_sem.at[2]
    )
    own_out.start()

    def sent(k, carry):
        i = plane_peer(k)
        g_copy(i, ing).wait_send()
        pack_copy(i, ing).wait_send()
        return carry

    lax.fori_loop(1, RING, sent, 0)

    def sent_pairs(k, carry):
        i, c = plane_peer(k // 2), (core + k) % 2
        red_copy(i, c, me).wait_send()
        return carry

    lax.fori_loop(1, PEERS, sent_pairs, 0)

    for mine in range(2):

        @pl.when(core == mine)
        def _():
            def sent_op(k, carry):
                i, c = plane_peer(k // 2), (core + k) % 2
                op_copy(i, c, ing, mine).wait_send()
                return carry

            lax.fori_loop(1, PEERS, sent_op, 0)

    def sent_z(k, carry):
        z_copy((z + k) % DEPTH, z).wait_send()
        return carry

    lax.fori_loop(1, DEPTH, sent_z, 0)

    own_out.wait()

    def out_wait(k, carry):
        j = plane_peer(RING - k)
        out_copy(ing, j).wait_recv()
        out_copy(j, ing).wait_send()
        return carry

    lax.fori_loop(1, RING, out_wait, 0)
    result[...] = out_recv[...]


def expand_kernel(folded, pair_key, own_wide, col_wide, update):
    for a in range(update.shape[0]):
        for s in range(GROUP_PAIRS // 8):
            pairs = slice(8 * s, 8 * (s + 1))
            wanted = pair_key[pairs, :] ^ own_wide[8 * a : 8 * (a + 1), :]
            values = folded[a, pairs, :].astype(F32)
            for t in range(TILES):
                width = min(LANES, NV - LANES * t)
                kept = jnp.where(wanted == col_wide[8 * t : 8 * (t + 1), :], values, 0.0)
                update[a, pairs, LANES * t : LANES * t + width] = kept[:, 0:width]


def body(amplitudes, integrals, fock_block, virtual_irrep, pair_irrep, pair_energy, virtual_energy):
    vmem = pl.BlockSpec(memory_space=pltpu.VMEM)
    smem = pl.BlockSpec(memory_space=pltpu.SMEM)
    hbm = pl.BlockSpec(memory_space=pl.ANY)
    dma = pltpu.SemaphoreType.DMA
    result, pair_key, own_wide, col_wide = pl.pallas_call(
        main_kernel,
        name="residual",
        out_shape=(
            jax.ShapeDtypeStruct((ROWS, GROUP_PAIRS, LANES), BF16),
            jax.ShapeDtypeStruct((GROUP_PAIRS, LANES), I32),
            jax.ShapeDtypeStruct((ROWS * 8, LANES), I32),
            jax.ShapeDtypeStruct((TILES * 8, LANES), I32),
        ),
        in_specs=[hbm, hbm, vmem, vmem, vmem, smem, smem],
        out_specs=(vmem, vmem, vmem, vmem),
        scratch_shapes=[
            pltpu.VMEM((HALVES, ROWS, GROUP, NV), BF16),
            pltpu.VMEM((HALVES, ROWS, GROUP, NV), BF16),
            pltpu.VMEM((8, LANES), I32),
            pltpu.VMEM((TILES * GROUP, LANES), BF16),
            pltpu.VMEM((8, LANES), F32),
            pltpu.VMEM((PADDED, LANES), I32),
            pltpu.VMEM((PADDED, LANES), F32),
            pltpu.VMEM((WIDE, LANES), I32),
            pltpu.VMEM((GROUP_PAIRS, LANES), I32),
            pltpu.VMEM((OWN, LANES), I32),
            pltpu.VMEM((RING, OWN, LANES), I32),
            pltpu.VMEM((2, ROWS, GROUP_PAIRS, LANES), BF16),
            pltpu.VMEM((2, NV, OWN, LANES), BF16),
            pltpu.VMEM((OWN * NV, LANES), F32),
            pltpu.VMEM((PADDED, 2 * LANES), BF16),
            pltpu.VMEM((OWN, PADDED, 2 * LANES), BF16),
            pltpu.VMEM((PADDED, 2 * LANES), BF16),
            pltpu.VMEM((2 * SLOT, LANES), F32),
            pltpu.VMEM((PADDED, LANES), F32),
            pltpu.VMEM((PEERS, SLOT, LANES), F32),
            pltpu.VMEM((SLOT, LANES), F32),
            pltpu.VMEM((DEPTH, SLOT, LANES), F32),
            pltpu.VMEM((SLOT, LANES), BF16),
            pltpu.VMEM((NV, LANES), BF16),
            pltpu.VMEM((OWN, PADDED, LANES), F32),
            pltpu.VMEM((NV, OWN, LANES), BF16),
            pltpu.VMEM((ROWS, GROUP_PAIRS, LANES), BF16),
            dma((HALVES,)), dma((HALVES,)), dma((RING,)), dma((RING,)), dma((RING,)), dma((RING,)),
            dma((PEERS,)), dma((PEERS,)), dma((DEPTH,)), dma((DEPTH,)), dma((PEERS,)), dma((PEERS,)),
            dma((RING,)), dma((RING,)), dma((3,)),
        ],
        compiler_params=pltpu.CompilerParams(collective_id=0, has_side_effects=True),
    )(
        jnp.transpose(amplitudes, (1, 0, 2)), jnp.transpose(integrals, (1, 0, 2)), fock_block,
        virtual_irrep, virtual_energy, pair_irrep, pair_energy,
    )

    step = 25
    update = pl.pallas_call(
        expand_kernel,
        name="expand",
        grid=(ROWS // step,),
        out_shape=jax.ShapeDtypeStruct((ROWS, GROUP_PAIRS, NV), F32),
        in_specs=[
            pl.BlockSpec((step, GROUP_PAIRS, LANES), lambda j: (j, 0, 0)),
            pl.BlockSpec((GROUP_PAIRS, LANES), lambda j: (0, 0)),
            pl.BlockSpec((step * 8, LANES), lambda j: (j, 0)),
            pl.BlockSpec((TILES * 8, LANES), lambda j: (0, 0)),
        ],
        out_specs=pl.BlockSpec((step, GROUP_PAIRS, NV), lambda j: (j, 0, 0)),
    )(result, pair_key, own_wide, col_wide)
    return jnp.transpose(update, (1, 0, 2))


def solution(mesh):
    in_specs = (
        P("grp", "ing", None),
        P("grp", "ing", None),
        P("ing", None),
        P(),
        P(("grp", "ing")),
        P(("grp", "ing")),
        P(),
    )
    out_specs = P("grp", "ing", None)
    return jax.shard_map(body, mesh=mesh, in_specs=in_specs, out_specs=out_specs, check_vma=False)
```

time: 66.5 us -> 65.5 us (0.985)
  Pallas kernels: 66.3 us -> 65.4 us
    pallas_call x1, Pallas kernels: 62.6 us -> 61.6 us  [body(): pl.pallas_call(main_kernel, name='residual', out_shape=(jax.ShapeDtypeStr...]
where the time goes in v3:
time: 65.5 us; the launch traced here: 65.4 us
  Pallas kernels  65.4 us (100%)
    pallas_call x1, Pallas kernels, body(): pl.pallas_call(main_kernel, name='residual', out_shape=(jax.ShapeDtypeStr...  61.6 us
    pallas_call x1, Pallas kernels, body(): pl.pallas_call(expand_kernel, name='expand', grid=(ROWS // step,), out_sh...  3.75 us

profile of v3, /device:TPU:1, one launch (start us, length us, event | category | flops | bytes accessed | tf_op | source)
XLA Modules:
  0.0 65.4 jit_solution(13675588555355741272)
XLA Ops:
  0.0 61.6 %residual.1 = (bf16[50,32,128]{2,1,0:T(8,128)(2,1)}, s32[32,128]{1,0:T(8,128)}, s32[400,128]{1,0:T(8,128)}, s32[56,128]{1,0:T(8,128)}) custom-call(bf16[50,32,800]{2,1,0:T(8,128)(2,1)} %bitcast.3, bf16[50,32,800]{2,1,0:T(8,128)(2,1)} %bitcast.4, bf16[50,800]{1,0:T(8,128)(2,1)} %fock.1, s32[800]{0:T(1024)} %irrep.1, f32[800]{0:T(1024)} %energy.1, ...), custom_call_target="tpu_custom_call" | custom-call | tf_op jit(solution)/shard_map/residual/pallas_call | solution.py:434
  61.6 3.7 %expand.1 = f32[50,32,800]{2,1,0:T(8,128)} custom-call(bf16[50,32,128]{2,1,0:T(8,128)(2,1)} %get-tuple-element.9.folded, s32[32,128]{1,0:T(8,128)} %get-tuple-element.10.pair_key, s32[400,128]{1,0:T(8,128)} %get-tuple-element.11.own_wide, s32[56,128]{1,0:T(8,128)} %get-tuple-element.12.col_wide), custom_call_target="tpu_custom_call" | custom-call | tf_op jit(solution)/shard_map/expand/pallas_call | solution.py:484

commit v4 on v3

--- a/solution.py
+++ b/solution.py
@@ -30,25 +30,30 @@
 
 
 def main_kernel(
-    amps, ints, fock, irrep, energy, pair_irrep, pair_energy,
+    amps, ints, fock_in, irrep_in, energy_in, pair_irrep_in, pair_energy_in,
     result, pair_key_out, own_wide_out, col_wide_out,
+    fock, irrep, energy, pair_irrep, pair_energy, own_wide, col_wide,
     amp_in, int_in, col_key, col_half, col_energy, row_key, row_energy, own_key, pair_key,
     g_send, g_recv, fold, pack_recv, mixed, lhs, rhs, int_rhs,
     fock_fold, corr, red_recv, z_send, z_recv, op_send, op_all,
     inverse, out_send, out_recv,
     amp_sem, int_sem, g_ssem, g_rsem, p_ssem, p_rsem, r_ssem, r_rsem,
-    z_ssem, z_rsem, o_ssem, o_rsem, t_ssem, t_rsem, own_sem,
+    z_ssem, z_rsem, o_ssem, o_rsem, t_ssem, t_rsem, own_sem, in_sem, key_sem,
 ):
     grp, ing = lax.axis_index("grp"), lax.axis_index("ing")
     z, core = grp // 2, grp % 2
     y, x = ing // SIDE, ing % SIDE
     me = ing * 2 + core
 
-    def plane_peer(k):
-        return ((y + k // SIDE) % SIDE) * SIDE + (x + k % SIDE) % SIDE
-
-    def far_peer(k):
-        return ((y + 2 + k // SIDE) % SIDE) * SIDE + (x + 2 + k % SIDE) % SIDE
+    beside = y + 1 - 2 * (y % 2)
+    across = [y, beside, (y + 2) % SIDE, (beside + 2) % SIDE]
+    along = [(x + k) % SIDE for k in range(SIDE)]
+    peer = {(r, k): across[r] * SIDE + along[k] for r in range(SIDE) for k in range(SIDE)}
+    hops = {(r, k): (0, 1, 2, 1)[r] + (0, 1, 2, 1)[k] for r in range(SIDE) for k in range(SIDE)}
+    near = [at for at in sorted(peer, key=hops.get) if at != (0, 0)]
+    far = near[::-1]
+    sibling = 1 - core
+    above = {k: (z + k) % DEPTH for k in (4, 3, 5, 2, 6, 1, 7)}
 
     def on_plane(i, c):
         return (z * 2 + c, i)
@@ -60,28 +65,33 @@
             pltpu.make_async_copy(ints.at[:, place], int_in.at[h], int_sem.at[h]),
         )
 
-    def load(k, carry):
-        for copy in chunk((y // 2 + k) % HALVES):
+    small = [
+        pltpu.make_async_copy(source, target, in_sem.at[n])
+        for n, (source, target) in enumerate(
+            ((pair_irrep_in, pair_irrep), (irrep_in, irrep), (energy_in, energy),
+             (pair_energy_in, pair_energy), (fock_in, fock))
+        )
+    ]
+    for copy in small:
+        copy.start()
+
+    barrier = pltpu.get_barrier_semaphore()
+
+    def greet(g, i):
+        pl.semaphore_signal(barrier, inc=1, device_id=(g, i), device_id_type=MESH)
+
+    for at in far:
+        greet(z * 2 + core, peer[at])
+        greet(z * 2 + sibling, peer[at])
+    greet(z * 2 + sibling, ing)
+    for k in above:
+        greet(above[k] * 2 + core, ing)
+
+    halves = [y // 2, 1 - y // 2]
+    for h in halves:
+        for copy in chunk(h):
             copy.start()
-        return carry
-
-    barrier = pltpu.get_barrier_semaphore()
-
-    def greet(k, carry):
-        pl.semaphore_signal(
-            barrier, inc=1, device_id=on_plane(plane_peer(k // 2), (core + k) % 2), device_id_type=MESH
-        )
-        return carry
-
-    def greet_z(k, carry):
-        pl.semaphore_signal(
-            barrier, inc=1, device_id=(((z + k) % DEPTH) * 2 + core, ing), device_id_type=MESH
-        )
-        return carry
-
-    lax.fori_loop(1, PEERS, greet, 0)
-    lax.fori_loop(1, DEPTH, greet_z, 0)
-    lax.fori_loop(0, HALVES, load, 0)
+    small[0].wait()
 
     for q in range(OWN):
         g_send[q : q + 1, :] = jnp.full((1, LANES), pair_irrep[q], I32)
@@ -95,11 +105,10 @@
             device_id=on_plane(i, core), device_id_type=MESH,
         )
 
-    def g_start(k, carry):
-        g_copy(plane_peer(k), ing).start()
-        return carry
-
-    lax.fori_loop(1, RING, g_start, 0)
+    for at in far:
+        g_copy(peer[at], ing).start()
+    for copy in small[1:]:
+        copy.wait()
 
     for t in range(TILES):
         if t < TILES - 1:
@@ -110,7 +119,7 @@
             col_key[t : t + 1, 0 : NV - LANES * t] = irrep[LANES * t : NV].reshape(1, NV - LANES * t)
             col_energy[t : t + 1, :] = jnp.zeros((1, LANES), F32)
             col_energy[t : t + 1, 0 : NV - LANES * t] = energy[LANES * t : NV].reshape(1, NV - LANES * t)
-        col_wide_out[8 * t : 8 * (t + 1), :] = jnp.broadcast_to(col_key[t : t + 1, :], (8, LANES))
+        col_wide[8 * t : 8 * (t + 1), :] = jnp.broadcast_to(col_key[t : t + 1, :], (8, LANES))
         col_half[GROUP * t : GROUP * (t + 1), :] = jnp.broadcast_to(
             col_key[t : t + 1, :].astype(F32), (GROUP, LANES)
         ).astype(BF16)
@@ -120,7 +129,7 @@
         row_key[place, :] = keys.T.astype(I32)
     own_key[...] = row_key[pl.ds(ROWS * ing, WIDE), :]
     for a in range(ROWS):
-        own_wide_out[8 * a : 8 * (a + 1), :] = jnp.broadcast_to(own_key[a : a + 1, :], (8, LANES))
+        own_wide[8 * a : 8 * (a + 1), :] = jnp.broadcast_to(own_key[a : a + 1, :], (8, LANES))
 
     def pack_copy(i, slot):
         return pltpu.make_async_remote_copy(
@@ -136,7 +145,7 @@
         def some_rows(b, carry):
             for a in range(ROWS // 10):
                 row = b * (ROWS // 10) + a
-                key = own_wide_out[pl.ds(pl.multiple_of(8 * row, 8), 8), :]
+                key = own_wide[pl.ds(pl.multiple_of(8 * row, 8), 8), :]
                 wanted = (jnp.concatenate([key, key], axis=0) ^ pairs).astype(F32).astype(BF16)
                 for which, source in ((0, amp_in), (1, int_in)):
                     folded = jnp.zeros((GROUP, LANES), BF16)
@@ -152,34 +161,28 @@
         fold.at[:, :, pl.ds(OWN * ing, OWN), :], pack_recv.at[:, pl.ds(ROWS * ing, ROWS)], own_sem.at[0]
     )
 
-    def pack_step(k, carry):
-        h = (y // 2 + k) % HALVES
-        for i in range(RING // HALVES):
-            j = RING // HALVES * h + i
-
-            @pl.when(j != ing)
-            def _():
-                g_copy(ing, j).wait_recv()
-
-            pair_key[pl.ds(OWN * j, OWN), :] = g_recv[j]
+    for n, h in enumerate(halves):
+        members = [at for at in near if at[0] // 2 == n]
+        if n == 0:
+            pair_key[pl.ds(OWN * ing, OWN), :] = g_recv[ing]
+        for at in members:
+            g_copy(ing, peer[at]).wait_recv()
+            pair_key[pl.ds(OWN * peer[at], OWN), :] = g_recv[peer[at]]
         for copy in chunk(h):
             copy.wait()
         fold_rows(h)
-        for i in range(RING // HALVES):
-            j = RING // HALVES * h + i
-
-            @pl.when(j != ing)
-            def _():
-                pack_copy(j, ing).start()
-
-            @pl.when(j == ing)
-            def _():
-                own_rows.start()
-
-        return carry
-
-    lax.fori_loop(0, HALVES, pack_step, 0)
-    pair_key_out[...] = pair_key[...]
+        for at in members[::-1]:
+            pack_copy(peer[at], ing).start()
+        if n == 0:
+            own_rows.start()
+    keys_out = [
+        pltpu.make_async_copy(source, target, key_sem.at[n])
+        for n, (source, target) in enumerate(
+            ((pair_key, pair_key_out), (own_wide, own_wide_out), (col_wide, col_wide_out))
+        )
+    ]
+    for copy in keys_out:
+        copy.start()
 
     fock_rows = fock[...].astype(F32)
     fock_keys = own_key[0:ROWS, :]
@@ -205,11 +208,8 @@
 
     own_rows.wait()
 
-    def pack_wait(k, carry):
-        pack_copy(ing, plane_peer(RING - k)).wait_recv()
-        return carry
-
-    lax.fori_loop(1, RING, pack_wait, 0)
+    for at in near:
+        pack_copy(ing, peer[at]).wait_recv()
     for which, target in ((0, lhs), (1, int_rhs)):
         mixed[...] = pack_recv[which].reshape(OWN * NV, LANES).astype(F32)
         for q in range(OWN):
@@ -235,28 +235,19 @@
             device_id_type=MESH,
         )
 
-    def red_step(k, carry):
-        for c in range(2):
-            i = far_peer(k)
-
-            @pl.when(i * 2 + c != me)
-            def _():
-                red_copy(i, c, me).start()
-
-        return carry
-
-    lax.fori_loop(0, RING, red_step, 0)
+    for at in far:
+        red_copy(peer[at], core, me).start()
+        red_copy(peer[at], sibling, me).start()
+    red_copy(ing, sibling, me).start()
     red_recv[me, 0:SLICE, :] = corr[pl.ds(ROWS * ing + SLICE * core, SLICE), :]
 
     for q in range(OWN):
         rhs[q, 0:NV, LANES : 2 * LANES] = -lhs[0:NV, LANES * q : LANES * (q + 1)]
 
-    def red_wait(k, carry):
-        i, c = plane_peer(k // 2), (core + k) % 2
-        red_copy(ing, core, i * 2 + c).wait_recv()
-        return carry
-
-    lax.fori_loop(1, PEERS, red_wait, 0)
+    red_copy(ing, core, ing * 2 + sibling).wait_recv()
+    for at in near:
+        for c in range(2):
+            red_copy(ing, core, peer[at] * 2 + c).wait_recv()
     total = red_recv[0, 0:SLICE, :]
     for w in range(1, PEERS):
         total = total + red_recv[w, 0:SLICE, :]
@@ -268,19 +259,12 @@
             recv_sem=z_rsem.at[slot], device_id=(dest * 2 + core, ing), device_id_type=MESH,
         )
 
-    def z_start(k, carry):
-        z_copy((z + 3 + k) % DEPTH, z).start()
-        return carry
-
-    lax.fori_loop(1, 5, z_start, 0)
-    lax.fori_loop(6, 9, z_start, 0)
+    for k in above:
+        z_copy(above[k], z).start()
     z_recv[z, 0:SLICE, :] = total
 
-    def z_wait(k, carry):
-        z_copy(z, (z + k) % DEPTH).wait_recv()
-        return carry
-
-    lax.fori_loop(1, DEPTH, z_wait, 0)
+    for k in above:
+        z_copy(z, above[k]).wait_recv()
     total = z_recv[0, 0:SLICE, :]
     for k in range(1, DEPTH):
         total = total + z_recv[k, 0:SLICE, :]
@@ -301,17 +285,10 @@
 
         @pl.when(core == mine)
         def _():
-            def op_start(k, carry):
+            for at in far:
                 for c in range(2):
-                    i = far_peer(k)
-
-                    @pl.when(i * 2 + c != me)
-                    def _():
-                        op_copy(i, c, ing, mine).start()
-
-                return carry
-
-            lax.fori_loop(0, RING, op_start, 0)
+                    op_copy(peer[at], c, ing, mine).start()
+            op_copy(ing, 1 - mine, ing, mine).start()
             own_op = pltpu.make_async_copy(
                 op_send.at[pl.ds(0, op_rows(mine))],
                 op_all.at[pl.ds(ROWS * ing + SLICE * mine, op_rows(mine))], own_sem.at[1],
@@ -319,17 +296,11 @@
             own_op.start()
             own_op.wait()
 
-    def op_wait(k, carry):
+            op_copy(ing, mine, ing, 1 - mine).wait_recv()
+
+    for at in near:
         for c in range(2):
-            i = plane_peer(k)
-
-            @pl.when(i * 2 + c != me)
-            def _():
-                op_copy(ing, core, i, c).wait_recv()
-
-        return carry
-
-    lax.fori_loop(0, RING, op_wait, 0)
+            op_copy(ing, core, peer[at], c).wait_recv()
 
     operator = op_all[...]
     for q in range(OWN):
@@ -355,62 +326,38 @@
             device_id_type=MESH,
         )
 
-    def out_step(k, carry):
-        j = far_peer(k)
-
-        @pl.when(j != ing)
-        def _():
-            out_copy(j, ing).start()
-
-        return carry
-
-    lax.fori_loop(0, RING, out_step, 0)
+    for at in far:
+        out_copy(peer[at], ing).start()
     own_out = pltpu.make_async_copy(
         out_send.at[pl.ds(ROWS * ing, ROWS)], out_recv.at[:, pl.ds(OWN * ing, OWN), :], own_sem.at[2]
     )
     own_out.start()
 
-    def sent(k, carry):
-        i = plane_peer(k)
-        g_copy(i, ing).wait_send()
-        pack_copy(i, ing).wait_send()
-        return carry
-
-    lax.fori_loop(1, RING, sent, 0)
-
-    def sent_pairs(k, carry):
-        i, c = plane_peer(k // 2), (core + k) % 2
-        red_copy(i, c, me).wait_send()
-        return carry
-
-    lax.fori_loop(1, PEERS, sent_pairs, 0)
-
+    for at in near:
+        g_copy(peer[at], ing).wait_send()
+        pack_copy(peer[at], ing).wait_send()
+        red_copy(peer[at], core, me).wait_send()
+        red_copy(peer[at], sibling, me).wait_send()
+    red_copy(ing, sibling, me).wait_send()
+    for k in above:
+        z_copy(above[k], z).wait_send()
     for mine in range(2):
 
         @pl.when(core == mine)
         def _():
-            def sent_op(k, carry):
-                i, c = plane_peer(k // 2), (core + k) % 2
-                op_copy(i, c, ing, mine).wait_send()
-                return carry
-
-            lax.fori_loop(1, PEERS, sent_op, 0)
-
-    def sent_z(k, carry):
-        z_copy((z + k) % DEPTH, z).wait_send()
-        return carry
-
-    lax.fori_loop(1, DEPTH, sent_z, 0)
-
+            for at in near:
+                for c in range(2):
+                    op_copy(peer[at], c, ing, mine).wait_send()
+            op_copy(ing, 1 - mine, ing, mine).wait_send()
+
+    for copy in keys_out:
+        copy.wait()
     own_out.wait()
 
-    def out_wait(k, carry):
-        j = plane_peer(RING - k)
-        out_copy(ing, j).wait_recv()
-        out_copy(j, ing).wait_send()
-        return carry
-
-    lax.fori_loop(1, RING, out_wait, 0)
+    for at in near:
+        out_copy(ing, peer[at]).wait_recv()
+    for at in near:
+        out_copy(peer[at], ing).wait_send()
     result[...] = out_recv[...]
 
 
@@ -428,7 +375,6 @@
 
 def body(amplitudes, integrals, fock_block, virtual_irrep, pair_irrep, pair_energy, virtual_energy):
     vmem = pl.BlockSpec(memory_space=pltpu.VMEM)
-    smem = pl.BlockSpec(memory_space=pltpu.SMEM)
     hbm = pl.BlockSpec(memory_space=pl.ANY)
     dma = pltpu.SemaphoreType.DMA
     result, pair_key, own_wide, col_wide = pl.pallas_call(
@@ -440,9 +386,16 @@
             jax.ShapeDtypeStruct((ROWS * 8, LANES), I32),
             jax.ShapeDtypeStruct((TILES * 8, LANES), I32),
         ),
-        in_specs=[hbm, hbm, vmem, vmem, vmem, smem, smem],
-        out_specs=(vmem, vmem, vmem, vmem),
+        in_specs=[hbm] * 7,
+        out_specs=(vmem, hbm, hbm, hbm),
         scratch_shapes=[
+            pltpu.VMEM((ROWS, NV), BF16),
+            pltpu.VMEM((NV,), I32),
+            pltpu.VMEM((NV,), F32),
+            pltpu.SMEM((OWN,), I32),
+            pltpu.SMEM((OWN,), F32),
+            pltpu.VMEM((ROWS * 8, LANES), I32),
+            pltpu.VMEM((TILES * 8, LANES), I32),
             pltpu.VMEM((HALVES, ROWS, GROUP, NV), BF16),
             pltpu.VMEM((HALVES, ROWS, GROUP, NV), BF16),
             pltpu.VMEM((8, LANES), I32),
@@ -472,7 +425,7 @@
             pltpu.VMEM((ROWS, GROUP_PAIRS, LANES), BF16),
             dma((HALVES,)), dma((HALVES,)), dma((RING,)), dma((RING,)), dma((RING,)), dma((RING,)),
             dma((PEERS,)), dma((PEERS,)), dma((DEPTH,)), dma((DEPTH,)), dma((PEERS,)), dma((PEERS,)),
-            dma((RING,)), dma((RING,)), dma((3,)),
+            dma((RING,)), dma((RING,)), dma((3,)), dma((5,)), dma((3,)),
         ],
         compiler_params=pltpu.CompilerParams(collective_id=0, has_side_effects=True),
     )(

time: 65.5 us -> 61.2 us (0.934)
  Pallas kernels: 65.4 us -> 61.1 us
    pallas_call x1, Pallas kernels: 61.6 us -> 57.3 us  [body(): pl.pallas_call(main_kernel, name='residual', out_shape=(jax.ShapeDtypeStr...]
where the time goes in v4:
time: 61.2 us; the launch traced here: 61.1 us
  Pallas kernels  61.1 us (100%)
    pallas_call x1, Pallas kernels, body(): pl.pallas_call(main_kernel, name='residual', out_shape=(jax.ShapeDtypeStr...  57.3 us
    pallas_call x1, Pallas kernels, body(): pl.pallas_call(expand_kernel, name='expand', grid=(ROWS // step,), out_sh...  3.75 us

profile of v4, /device:TPU:1, one launch (start us, length us, event | category | flops | bytes accessed | tf_op | source)
XLA Modules:
  0.0 61.1 jit_solution(8431553911512474566)
XLA Ops:
  0.0 57.3 %residual.1 = (bf16[50,32,128]{2,1,0:T(8,128)(2,1)}, s32[32,128]{1,0:T(8,128)}, s32[400,128]{1,0:T(8,128)}, s32[56,128]{1,0:T(8,128)}) custom-call(bf16[50,32,800]{2,1,0:T(8,128)(2,1)} %bitcast.3, bf16[50,32,800]{2,1,0:T(8,128)(2,1)} %bitcast.4, bf16[50,800]{1,0:T(8,128)(2,1)} %fock_in.1, s32[800]{0:T(1024)} %irrep_in.1, f32[800]{0:T(1024)} %energy_in.1, ...), custom_call_target="tpu_custom_call" | custom-call | tf_op jit(solution)/shard_map/residual/pallas_call | solution.py:380
  57.3 3.7 %expand.1 = f32[50,32,800]{2,1,0:T(8,128)} custom-call(bf16[50,32,128]{2,1,0:T(8,128)(2,1)} %get-tuple-element.9.folded, s32[32,128]{1,0:T(8,128)} %get-tuple-element.10.pair_key, s32[400,128]{1,0:T(8,128)} %get-tuple-element.11.own_wide, s32[56,128]{1,0:T(8,128)} %get-tuple-element.12.col_wide), custom_call_target="tpu_custom_call" | custom-call | tf_op jit(solution)/shard_map/expand/pallas_call | solution.py:437

commit v5 on v4

--- a/solution.py
+++ b/solution.py
@@ -36,7 +36,7 @@
     amp_in, int_in, col_key, col_half, col_energy, row_key, row_energy, own_key, pair_key,
     g_send, g_recv, fold, pack_recv, mixed, lhs, rhs, int_rhs,
     fock_fold, corr, red_recv, z_send, z_recv, op_send, op_all,
-    inverse, out_send, out_recv,
+    inverse, out_send,
     amp_sem, int_sem, g_ssem, g_rsem, p_ssem, p_rsem, r_ssem, r_rsem,
     z_ssem, z_rsem, o_ssem, o_rsem, t_ssem, t_rsem, own_sem, in_sem, key_sem,
 ):
@@ -87,10 +87,9 @@
     for k in above:
         greet(above[k] * 2 + core, ing)
 
-    halves = [y // 2, 1 - y // 2]
-    for h in halves:
-        for copy in chunk(h):
-            copy.start()
+    halves = [1 - y // 2, y // 2]
+    for copy in chunk(halves[0]):
+        copy.start()
     small[0].wait()
 
     for q in range(OWN):
@@ -107,6 +106,8 @@
 
     for at in far:
         g_copy(peer[at], ing).start()
+    for copy in chunk(halves[1]):
+        copy.start()
     for copy in small[1:]:
         copy.wait()
 
@@ -162,8 +163,8 @@
     )
 
     for n, h in enumerate(halves):
-        members = [at for at in near if at[0] // 2 == n]
-        if n == 0:
+        members = [at for at in near if at[0] // 2 != n]
+        if n == 1:
             pair_key[pl.ds(OWN * ing, OWN), :] = g_recv[ing]
         for at in members:
             g_copy(ing, peer[at]).wait_recv()
@@ -173,7 +174,7 @@
         fold_rows(h)
         for at in members[::-1]:
             pack_copy(peer[at], ing).start()
-        if n == 0:
+        if n == 1:
             own_rows.start()
     keys_out = [
         pltpu.make_async_copy(source, target, key_sem.at[n])
@@ -321,7 +322,7 @@
 
     def out_copy(i, slot):
         return pltpu.make_async_remote_copy(
-            src_ref=out_send.at[pl.ds(ROWS * i, ROWS)], dst_ref=out_recv.at[:, pl.ds(OWN * slot, OWN), :],
+            src_ref=out_send.at[pl.ds(ROWS * i, ROWS)], dst_ref=result.at[:, pl.ds(OWN * slot, OWN), :],
             send_sem=t_ssem.at[i], recv_sem=t_rsem.at[slot], device_id=on_plane(i, core),
             device_id_type=MESH,
         )
@@ -329,7 +330,7 @@
     for at in far:
         out_copy(peer[at], ing).start()
     own_out = pltpu.make_async_copy(
-        out_send.at[pl.ds(ROWS * ing, ROWS)], out_recv.at[:, pl.ds(OWN * ing, OWN), :], own_sem.at[2]
+        out_send.at[pl.ds(ROWS * ing, ROWS)], result.at[:, pl.ds(OWN * ing, OWN), :], own_sem.at[2]
     )
     own_out.start()
 
@@ -358,7 +359,6 @@
         out_copy(ing, peer[at]).wait_recv()
     for at in near:
         out_copy(peer[at], ing).wait_send()
-    result[...] = out_recv[...]
 
 
 def expand_kernel(folded, pair_key, own_wide, col_wide, update):
@@ -374,7 +374,6 @@
 
 
 def body(amplitudes, integrals, fock_block, virtual_irrep, pair_irrep, pair_energy, virtual_energy):
-    vmem = pl.BlockSpec(memory_space=pltpu.VMEM)
     hbm = pl.BlockSpec(memory_space=pl.ANY)
     dma = pltpu.SemaphoreType.DMA
     result, pair_key, own_wide, col_wide = pl.pallas_call(
@@ -387,7 +386,7 @@
             jax.ShapeDtypeStruct((TILES * 8, LANES), I32),
         ),
         in_specs=[hbm] * 7,
-        out_specs=(vmem, hbm, hbm, hbm),
+        out_specs=(hbm, hbm, hbm, hbm),
         scratch_shapes=[
             pltpu.VMEM((ROWS, NV), BF16),
             pltpu.VMEM((NV,), I32),
@@ -422,7 +421,6 @@
             pltpu.VMEM((NV, LANES), BF16),
             pltpu.VMEM((OWN, PADDED, LANES), F32),
             pltpu.VMEM((NV, OWN, LANES), BF16),
-            pltpu.VMEM((ROWS, GROUP_PAIRS, LANES), BF16),
             dma((HALVES,)), dma((HALVES,)), dma((RING,)), dma((RING,)), dma((RING,)), dma((RING,)),
             dma((PEERS,)), dma((PEERS,)), dma((DEPTH,)), dma((DEPTH,)), dma((PEERS,)), dma((PEERS,)),
             dma((RING,)), dma((RING,)), dma((3,)), dma((5,)), dma((3,)),

time: 61.2 us -> 58.9 us (0.962)
  Pallas kernels: 61.1 us -> 58.8 us
    pallas_call x1, Pallas kernels: 57.3 us -> 55.1 us  [body(): pl.pallas_call(main_kernel, name='residual', out_shape=(jax.ShapeDtypeStr...]
where the time goes in v5:
time: 58.9 us; the launch traced here: 58.8 us
  Pallas kernels  58.8 us (100%)
    pallas_call x1, Pallas kernels, body(): pl.pallas_call(main_kernel, name='residual', out_shape=(jax.ShapeDtypeStr...  55.1 us
    pallas_call x1, Pallas kernels, body(): pl.pallas_call(expand_kernel, name='expand', grid=(ROWS // step,), out_sh...  3.75 us

profile of v5, /device:TPU:1, one launch (start us, length us, event | category | flops | bytes accessed | tf_op | source)
XLA Modules:
  0.0 58.8 jit_solution(5094113186724876204)
XLA Ops:
  0.0 55.1 %residual.1 = (bf16[50,32,128]{2,1,0:T(8,128)(2,1)}, s32[32,128]{1,0:T(8,128)}, s32[400,128]{1,0:T(8,128)}, s32[56,128]{1,0:T(8,128)}) custom-call(bf16[50,32,800]{2,1,0:T(8,128)(2,1)} %bitcast.3, bf16[50,32,800]{2,1,0:T(8,128)(2,1)} %bitcast.4, bf16[50,800]{1,0:T(8,128)(2,1)} %fock_in.1, s32[800]{0:T(1024)} %irrep_in.1, f32[800]{0:T(1024)} %energy_in.1, ...), custom_call_target="tpu_custom_call" | custom-call | tf_op jit(solution)/shard_map/residual/pallas_call | solution.py:379
  55.1 3.7 %expand.1 = f32[50,32,800]{2,1,0:T(8,128)} custom-call(bf16[50,32,128]{2,1,0:T(8,128)(2,1)} %get-tuple-element.9.folded, s32[32,128]{1,0:T(8,128)} %get-tuple-element.10.pair_key, s32[400,128]{1,0:T(8,128)} %get-tuple-element.11.own_wide, s32[56,128]{1,0:T(8,128)} %get-tuple-element.12.col_wide), custom_call_target="tpu_custom_call" | custom-call | tf_op jit(solution)/shard_map/expand/pallas_call | solution.py:435

commit v6 on v5

--- a/solution.py
+++ b/solution.py
@@ -172,10 +172,9 @@
         for copy in chunk(h):
             copy.wait()
         fold_rows(h)
-        for at in members[::-1]:
-            pack_copy(peer[at], ing).start()
-        if n == 1:
-            own_rows.start()
+    for at in far:
+        pack_copy(peer[at], ing).start()
+    own_rows.start()
     keys_out = [
         pltpu.make_async_copy(source, target, key_sem.at[n])
         for n, (source, target) in enumerate(
@@ -303,22 +302,8 @@
         for c in range(2):
             op_copy(ing, core, peer[at], c).wait_recv()
 
-    operator = op_all[...]
     for q in range(OWN):
-        rhs[q, 0:NV, 0:LANES] = operator
-        left = jnp.concatenate([lhs[0:NV, LANES * q : LANES * (q + 1)], operator], axis=1)
-        keys = row_key[0:NV, :] ^ pair_irrep[q]
-        folded = jnp.zeros((NV, LANES), F32)
-        for t in range(0, TILES, 2):
-            width = min(2, TILES - t)
-            block = lax.dot_general(
-                left, rhs[q, LANES * t : LANES * (t + width), :], NT, preferred_element_type=F32
-            )
-            for u in range(width):
-                part = block[:, LANES * u : LANES * (u + 1)]
-                folded = jnp.where(keys == col_key[t + u : t + u + 1, :], part, folded)
-        mixed[pl.ds(q, NV, stride=OWN), :] = folded * inverse[q, 0:NV, :]
-    out_send[...] = mixed[...].astype(BF16).reshape(NV, OWN, LANES)
+        rhs[q, 0:NV, 0:LANES] = op_all[...]
 
     def out_copy(i, slot):
         return pltpu.make_async_remote_copy(
@@ -327,8 +312,26 @@
             device_id_type=MESH,
         )
 
-    for at in far:
-        out_copy(peer[at], ing).start()
+    count = NV // HALVES
+    for n, h in enumerate(halves):
+        place = pl.ds(pl.multiple_of(count * h, count), count)
+        for q in range(OWN):
+            left = jnp.concatenate([lhs[place, LANES * q : LANES * (q + 1)], op_all[place, :]], axis=1)
+            keys = row_key[place, :] ^ pair_irrep[q]
+            folded = jnp.zeros((count, LANES), F32)
+            for t in range(0, TILES, 2):
+                width = min(2, TILES - t)
+                block = lax.dot_general(
+                    left, rhs[q, LANES * t : LANES * (t + width), :], NT, preferred_element_type=F32
+                )
+                for u in range(width):
+                    part = block[:, LANES * u : LANES * (u + 1)]
+                    folded = jnp.where(keys == col_key[t + u : t + u + 1, :], part, folded)
+            mixed[pl.ds(q, count, stride=OWN), :] = folded * inverse[q, place, :]
+        out_send[place] = mixed[0 : OWN * count, :].astype(BF16).reshape(count, OWN, LANES)
+        for at in far:
+            if at[0] // 2 != n:
+                out_copy(peer[at], ing).start()
     own_out = pltpu.make_async_copy(
         out_send.at[pl.ds(ROWS * ing, ROWS)], result.at[:, pl.ds(OWN * ing, OWN), :], own_sem.at[2]
     )

time: 58.9 us -> 58 us (0.985)
  Pallas kernels: 58.8 us -> 57.9 us
    pallas_call x1, Pallas kernels: 55.1 us -> 54.2 us  [body(): pl.pallas_call(main_kernel, name='residual', out_shape=(jax.ShapeDtypeStr...]
where the time goes in v6:
time: 58 us; the launch traced here: 57.9 us
  Pallas kernels  57.9 us (100%)
    pallas_call x1, Pallas kernels, body(): pl.pallas_call(main_kernel, name='residual', out_shape=(jax.ShapeDtypeStr...  54.2 us
    pallas_call x1, Pallas kernels, body(): pl.pallas_call(expand_kernel, name='expand', grid=(ROWS // step,), out_sh...  3.75 us

profile of v6, /device:TPU:1, one launch (start us, length us, event | category | flops | bytes accessed | tf_op | source)
XLA Modules:
  0.0 57.9 jit_solution(13176152335816635034)
XLA Ops:
  0.0 54.2 %residual.1 = (bf16[50,32,128]{2,1,0:T(8,128)(2,1)}, s32[32,128]{1,0:T(8,128)}, s32[400,128]{1,0:T(8,128)}, s32[56,128]{1,0:T(8,128)}) custom-call(bf16[50,32,800]{2,1,0:T(8,128)(2,1)} %bitcast.3, bf16[50,32,800]{2,1,0:T(8,128)(2,1)} %bitcast.4, bf16[50,800]{1,0:T(8,128)(2,1)} %fock_in.1, s32[800]{0:T(1024)} %irrep_in.1, f32[800]{0:T(1024)} %energy_in.1, ...), custom_call_target="tpu_custom_call" | custom-call | tf_op jit(solution)/shard_map/residual/pallas_call | solution.py:382
  54.2 3.7 %expand.1 = f32[50,32,800]{2,1,0:T(8,128)} custom-call(bf16[50,32,128]{2,1,0:T(8,128)(2,1)} %get-tuple-element.9.folded, s32[32,128]{1,0:T(8,128)} %get-tuple-element.10.pair_key, s32[400,128]{1,0:T(8,128)} %get-tuple-element.11.own_wide, s32[56,128]{1,0:T(8,128)} %get-tuple-element.12.col_wide), custom_call_target="tpu_custom_call" | custom-call | tf_op jit(solution)/shard_map/expand/pallas_call | solution.py:438

commit v7 on v6

--- a/solution.py
+++ b/solution.py
@@ -35,15 +35,14 @@
     fock, irrep, energy, pair_irrep, pair_energy, own_wide, col_wide,
     amp_in, int_in, col_key, col_half, col_energy, row_key, row_energy, own_key, pair_key,
     g_send, g_recv, fold, pack_recv, mixed, lhs, rhs, int_rhs,
-    fock_fold, corr, red_recv, z_send, z_recv, op_send, op_all,
+    fock_fold, corr, pair_recv, red_send, red_recv, z_send, z_recv, op_send, op_all,
     inverse, out_send,
-    amp_sem, int_sem, g_ssem, g_rsem, p_ssem, p_rsem, r_ssem, r_rsem,
+    amp_sem, int_sem, g_ssem, g_rsem, p_ssem, p_rsem, s_ssem, s_rsem, r_ssem, r_rsem,
     z_ssem, z_rsem, o_ssem, o_rsem, t_ssem, t_rsem, own_sem, in_sem, key_sem,
 ):
     grp, ing = lax.axis_index("grp"), lax.axis_index("ing")
     z, core = grp // 2, grp % 2
     y, x = ing // SIDE, ing % SIDE
-    me = ing * 2 + core
 
     beside = y + 1 - 2 * (y % 2)
     across = [y, beside, (y + 2) % SIDE, (beside + 2) % SIDE]
@@ -228,28 +227,39 @@
             folded = jnp.where(keys == col_key[t : t + 1, :], part, folded)
         corr[place, :] = folded
 
-    def red_copy(i, c, slot):
-        return pltpu.make_async_remote_copy(
-            src_ref=corr.at[pl.ds(ROWS * i + SLICE * c, SLICE)], dst_ref=red_recv.at[slot, pl.ds(0, SLICE)],
-            send_sem=r_ssem.at[i * 2 + c], recv_sem=r_rsem.at[slot], device_id=on_plane(i, c),
+    def pair_copy(i):
+        return pltpu.make_async_remote_copy(
+            src_ref=corr.at[pl.ds(ROWS * i + SLICE * sibling, SLICE)], dst_ref=pair_recv.at[i, pl.ds(0, SLICE)],
+            send_sem=s_ssem.at[i], recv_sem=s_rsem.at[i], device_id=on_plane(ing, sibling),
             device_id_type=MESH,
         )
 
-    for at in far:
-        red_copy(peer[at], core, me).start()
-        red_copy(peer[at], sibling, me).start()
-    red_copy(ing, sibling, me).start()
-    red_recv[me, 0:SLICE, :] = corr[pl.ds(ROWS * ing + SLICE * core, SLICE), :]
+    def red_copy(i, slot):
+        return pltpu.make_async_remote_copy(
+            src_ref=red_send.at[i, pl.ds(0, SLICE)], dst_ref=red_recv.at[slot, pl.ds(0, SLICE)],
+            send_sem=r_ssem.at[i], recv_sem=r_rsem.at[slot], device_id=on_plane(i, core),
+            device_id_type=MESH,
+        )
+
+    for at in far + [(0, 0)]:
+        pair_copy(peer[at]).start()
+    for at in far + [(0, 0)]:
+        i = peer[at]
+        pair_copy(i).wait_recv()
+        both = corr[pl.ds(ROWS * i + SLICE * core, SLICE), :] + pair_recv[i, 0:SLICE, :]
+        if at == (0, 0):
+            red_recv[i, 0:SLICE, :] = both
+        else:
+            red_send[i, 0:SLICE, :] = both
+            red_copy(i, ing).start()
 
     for q in range(OWN):
         rhs[q, 0:NV, LANES : 2 * LANES] = -lhs[0:NV, LANES * q : LANES * (q + 1)]
 
-    red_copy(ing, core, ing * 2 + sibling).wait_recv()
-    for at in near:
-        for c in range(2):
-            red_copy(ing, core, peer[at] * 2 + c).wait_recv()
+    for at in near:
+        red_copy(ing, peer[at]).wait_recv()
     total = red_recv[0, 0:SLICE, :]
-    for w in range(1, PEERS):
+    for w in range(1, RING):
         total = total + red_recv[w, 0:SLICE, :]
     z_send[0:SLICE, :] = total
 
@@ -340,9 +350,9 @@
     for at in near:
         g_copy(peer[at], ing).wait_send()
         pack_copy(peer[at], ing).wait_send()
-        red_copy(peer[at], core, me).wait_send()
-        red_copy(peer[at], sibling, me).wait_send()
-    red_copy(ing, sibling, me).wait_send()
+        red_copy(peer[at], ing).wait_send()
+    for at in peer:
+        pair_copy(peer[at]).wait_send()
     for k in above:
         z_copy(above[k], z).wait_send()
     for mine in range(2):
@@ -417,7 +427,9 @@
             pltpu.VMEM((PADDED, 2 * LANES), BF16),
             pltpu.VMEM((2 * SLOT, LANES), F32),
             pltpu.VMEM((PADDED, LANES), F32),
-            pltpu.VMEM((PEERS, SLOT, LANES), F32),
+            pltpu.VMEM((RING, SLOT, LANES), F32),
+            pltpu.VMEM((RING, SLOT, LANES), F32),
+            pltpu.VMEM((RING, SLOT, LANES), F32),
             pltpu.VMEM((SLOT, LANES), F32),
             pltpu.VMEM((DEPTH, SLOT, LANES), F32),
             pltpu.VMEM((SLOT, LANES), BF16),
@@ -425,7 +437,7 @@
             pltpu.VMEM((OWN, PADDED, LANES), F32),
             pltpu.VMEM((NV, OWN, LANES), BF16),
             dma((HALVES,)), dma((HALVES,)), dma((RING,)), dma((RING,)), dma((RING,)), dma((RING,)),
-            dma((PEERS,)), dma((PEERS,)), dma((DEPTH,)), dma((DEPTH,)), dma((PEERS,)), dma((PEERS,)),
+            dma((RING,)), dma((RING,)), dma((RING,)), dma((RING,)), dma((DEPTH,)), dma((DEPTH,)), dma((PEERS,)), dma((PEERS,)),
             dma((RING,)), dma((RING,)), dma((3,)), dma((5,)), dma((3,)),
         ],
         compiler_params=pltpu.CompilerParams(collective_id=0, has_side_effects=True),

time: 58 us -> 57.2 us (0.986)
  Pallas kernels: 57.9 us -> 57.1 us
    pallas_call x1, Pallas kernels: 54.2 us -> 53.3 us  [body(): pl.pallas_call(main_kernel, name='residual', out_shape=(jax.ShapeDtypeStr...]
where the time goes in v7:
time: 57.2 us; the launch traced here: 57.1 us
  Pallas kernels  57.1 us (100%)
    pallas_call x1, Pallas kernels, body(): pl.pallas_call(main_kernel, name='residual', out_shape=(jax.ShapeDtypeStr...  53.3 us
    pallas_call x1, Pallas kernels, body(): pl.pallas_call(expand_kernel, name='expand', grid=(ROWS // step,), out_sh...  3.75 us

profile of v7, /device:TPU:1, one launch (start us, length us, event | category | flops | bytes accessed | tf_op | source)
XLA Modules:
  0.0 57.1 jit_solution(2469045088216043670)
XLA Ops:
  0.0 53.3 %residual.1 = (bf16[50,32,128]{2,1,0:T(8,128)(2,1)}, s32[32,128]{1,0:T(8,128)}, s32[400,128]{1,0:T(8,128)}, s32[56,128]{1,0:T(8,128)}) custom-call(bf16[50,32,800]{2,1,0:T(8,128)(2,1)} %bitcast.3, bf16[50,32,800]{2,1,0:T(8,128)(2,1)} %bitcast.4, bf16[50,800]{1,0:T(8,128)(2,1)} %fock_in.1, s32[800]{0:T(1024)} %irrep_in.1, f32[800]{0:T(1024)} %energy_in.1, ...), custom_call_target="tpu_custom_call" | custom-call | tf_op jit(solution)/shard_map/residual/pallas_call | solution.py:392
  53.4 3.7 %expand.1 = f32[50,32,800]{2,1,0:T(8,128)} custom-call(bf16[50,32,128]{2,1,0:T(8,128)(2,1)} %get-tuple-element.9.folded, s32[32,128]{1,0:T(8,128)} %get-tuple-element.10.pair_key, s32[400,128]{1,0:T(8,128)} %get-tuple-element.11.own_wide, s32[56,128]{1,0:T(8,128)} %get-tuple-element.12.col_wide), custom_call_target="tpu_custom_call" | custom-call | tf_op jit(solution)/shard_map/expand/pallas_call | solution.py:450
